TPU v7x, 32 devices: a whole 2x2x4 slice. The times are simulated.
32 devices in a mesh: leaf: 4 (over x, core), row: 4 (over z), col: 2 (over y).
Axes of the slice: x: 2, y: 2, z: 4, core: 2. Of those that a mesh axis runs over, the one named last changes fastest.
Arguments:
- widths: int32 [15], replicated, may hold values from 1024 to 2048, as said below
- bottom_lists: int32 [8, 32], P('leaf'), may hold values from 0 to 47, as said below
- root_inverse: bfloat16 [2048, 2048], P('row')
- second_panels: bfloat16 [4, 2048, 1024], P('leaf', 'row', 'col'), may hold values from -0.09375 to 0.09375
- second_inverse: bfloat16 [4, 1024, 2048], P('leaf', 'col', 'row')
- third_panels: bfloat16 [4, 2, 2048, 2048], P('leaf', None, 'row', 'col'), may hold values from -0.09375 to 0.09375
- third_inverse: bfloat16 [4, 2048, 2048], P('leaf', 'col', 'row')
- bottom_panels: bfloat16 [8, 4096, 2048], P('leaf', 'row', 'col'), may hold values from -0.09375 to 0.09375
- bottom_inverse: bfloat16 [8, 2048, 2048], P('leaf', 'col', 'row')
Outputs:
- second_off: bfloat16 [4, 2048, 1024], P('leaf', 'row', 'col')
- second_diag: bfloat16 [4, 1024, 2048], P('leaf', 'col', 'row')
- third_off: bfloat16 [4, 2, 2048, 2048], P('leaf', None, 'row', 'col')
- third_diag: bfloat16 [4, 2048, 2048], P('leaf', 'col', 'row')
- bottom_off: bfloat16 [8, 3, 2048, 2048], P('leaf', None, 'row', 'col')
- bottom_diag: bfloat16 [8, 2048, 2048], P('leaf', 'col', 'row')
Inputs may be any that keep to these rules, and one draw needn't show every extreme that they name: `widths`: some supernode has 2048 columns and some 2048/2. `bottom_lists`: row e lists 32 different blocks of 128 rows of its chain (root, then second-level ancestor, then parent, 16 blocks each) in increasing order; block 0 and all blocks of the parent are always listed.
All inputs are finite; a program needn't handle non-finite values.
Results may differ from a plain program's by a relative error of at most 0.015.
Values may be sent and summed in bfloat16 or wider, within the bound.
No kernel may reach another device: no remote copies, remote signals or barrier semaphores. Data moves between devices by JAX's collectives and lax.ppermute only.
A program may use at most 192 MiB of HBM per device.

v0:
```python
import jax
import jax.numpy as jnp
from jax import lax
from jax.sharding import PartitionSpec as P

NODES = 15
BOTTOM = 8


def partner(block, axis, apart):
    count = lax.axis_size(axis)
    route = []
    for low in range(count):
        high = low | 1 << apart
        if high != low and high < count:
            route += [(low, high), (high, low)]
    return lax.ppermute(block, axis, route)


def node_width(widths, node_at):
    return jnp.sum(jnp.where(jnp.arange(widths.shape[0]) == node_at, widths, 0))


def chain_fold(flat_chain, tile_width, ancestors, shard_piece):
    piece_rows = shard_piece.shape[1]
    picked = jnp.concatenate(
        [
            lax.dynamic_slice_in_dim(flat_chain, level_at * tile_width, piece_rows, 1)
            for level_at in range(ancestors)
        ],
        axis=1,
    )
    stacked = shard_piece.reshape(ancestors * piece_rows, shard_piece.shape[2])
    return jnp.dot(picked, stacked, preferred_element_type=jnp.float32)


def local(
    widths,
    bottom_lists,
    root_inverse,
    second_panels,
    second_inverse,
    third_panels,
    third_inverse,
    bottom_panels,
    bottom_inverse,
):
    group_at = lax.axis_index("leaf")
    row_at = lax.axis_index("row")
    col_at = lax.axis_index("col")
    rows_dev = root_inverse.shape[0]
    tile_width = root_inverse.shape[1]
    half_cols = second_panels.shape[2]
    own_cols = third_panels.shape[3]
    half_at = group_at % 2
    parent_one = 1 + group_at // 2
    node_two = 3 + group_at
    row_first = row_at * rows_dev
    row_index = row_first + jnp.arange(rows_dev)
    root_width = node_width(widths, 0)
    root_mask = (row_index < root_width)[:, None] & (jnp.arange(tile_width) < root_width)[None, :]
    root_block = jnp.where(root_mask, root_inverse, 0)
    width_one = node_width(widths, parent_one)
    mask_rows_one = row_index < width_one
    first_col = half_at * (tile_width // 2) + col_at * half_cols
    mask_cols_one = first_col + jnp.arange(half_cols) < width_one
    panel_one = jnp.where(mask_cols_one[None, :], second_panels[0], 0)
    shard_piece = lax.all_gather(panel_one, "row", axis=0, tiled=True)
    flat_piece = shard_piece
    product_one = jnp.dot(root_block, flat_piece, preferred_element_type=jnp.float32)
    off_one = (-product_one).astype(jnp.bfloat16)
    mine_half = lax.all_gather(off_one, "col", axis=1, tiled=True)
    other_half = partner(mine_half, "leaf", 0)
    off_full = jnp.where(
        half_at == 0,
        jnp.concatenate([mine_half, other_half], 1),
        jnp.concatenate([other_half, mine_half], 1),
    )
    term_one = lax.dot_general(
        panel_one, off_full, (((0,), (0,)), ((), ())), preferred_element_type=jnp.float32
    )
    summed_one = lax.psum_scatter(
        term_one.astype(jnp.bfloat16), "row", scatter_dimension=1, tiled=True
    ).astype(jnp.float32)
    inverse_one = jnp.where(
        mask_cols_one[:, None] & mask_rows_one[None, :], second_inverse[0], 0
    ).astype(jnp.float32)
    diag_one = (inverse_one - summed_one).astype(jnp.bfloat16)
    mine_diag = lax.all_gather(diag_one.T, "col", axis=1, tiled=True)
    other_diag = partner(mine_diag, "leaf", 0)
    diag_full = jnp.where(
        half_at == 0,
        jnp.concatenate([mine_diag, other_diag], 1),
        jnp.concatenate([other_diag, mine_diag], 1),
    )
    second_off = off_one[None]
    second_diag = diag_one[None]
    turned_one = lax.all_to_all(off_full, "row", split_axis=1, concat_axis=0, tiled=True)
    chain_two = jnp.stack(
        [jnp.concatenate([root_block, off_full], 1), jnp.concatenate([turned_one.T, diag_full], 1)],
        0,
    )
    flat_two = chain_two.reshape(2 * rows_dev, 2 * tile_width)
    first_own = col_at * own_cols
    width_two = node_width(widths, node_two)
    mask_cols_two = first_own + jnp.arange(own_cols) < width_two
    panel_two = jnp.where(mask_cols_two[None, None, :], third_panels[0], 0)
    product_two = chain_fold(
        flat_two, tile_width, 2, lax.all_gather(panel_two, "row", axis=1, tiled=True)
    )
    off_two = (-product_two).astype(jnp.bfloat16).reshape(2, rows_dev, own_cols)
    full_two = lax.all_gather(off_two, "col", axis=2, tiled=True)
    term_two = jnp.einsum("kin,kim->nm", panel_two, full_two, preferred_element_type=jnp.float32)
    summed_two = lax.psum_scatter(
        term_two.astype(jnp.bfloat16), "row", scatter_dimension=1, tiled=True
    ).astype(jnp.float32)
    mask_rows_two = row_index < width_two
    inverse_two = jnp.where(
        mask_cols_two[:, None] & mask_rows_two[None, :], third_inverse[0], 0
    ).astype(jnp.float32)
    diag_two = (inverse_two - summed_two).astype(jnp.bfloat16)
    diag_rows_two = lax.all_gather(diag_two.T, "col", axis=1, tiled=True)
    turned_two = lax.all_to_all(full_two, "row", split_axis=2, concat_axis=1, tiled=True)
    lower_two = jnp.transpose(turned_two, (2, 0, 1)).reshape(rows_dev, 2 * tile_width)
    chain_three = jnp.stack(
        [
            jnp.concatenate([chain_two[0], full_two[0]], 1),
            jnp.concatenate([chain_two[1], full_two[1]], 1),
            jnp.concatenate([lower_two, diag_rows_two], 1),
        ],
        0,
    )
    flat_three = chain_three.reshape(3 * rows_dev, 3 * tile_width)
    bottom_dev = bottom_panels.shape[0]
    list_len = bottom_lists.shape[1]
    block_rows = 2 * tile_width // list_len
    node_three = NODES - BOTTOM + bottom_dev * group_at + jnp.arange(bottom_dev)
    width_three = jnp.sum(
        jnp.where(jnp.arange(widths.shape[0])[None, :] == node_three[:, None], widths[None, :], 0),
        1,
    )
    mask_cols_three = (first_own + jnp.arange(own_cols))[None, :] < width_three[:, None]
    panel_three = jnp.where(mask_cols_three[:, None, :], bottom_panels, 0)
    positions = (
        jnp.repeat(bottom_lists, block_rows, axis=1) * block_rows
        + jnp.arange(list_len * block_rows) % block_rows
    )
    own_chain = (jnp.arange(3)[:, None] * tile_width + row_index[None, :]).reshape(-1)
    matches = bottom_lists[:, :, None] == (own_chain // block_rows)[None, None, :]
    member = jnp.any(matches, axis=1)
    slot_index = (
        jnp.sum(jnp.where(matches, jnp.arange(list_len)[None, :, None], 0), axis=1) * block_rows
        + own_chain % block_rows
    )
    shard_piece = lax.all_gather(panel_three, "row", axis=1, tiled=True)
    kept_rows = jnp.zeros((bottom_dev, 3 * rows_dev, own_cols), jnp.bfloat16)
    piece_rows = shard_piece.shape[1]
    columns = jnp.take(flat_three, positions.reshape(-1), axis=1).reshape(
        3 * rows_dev, bottom_dev, piece_rows
    )
    running = jnp.einsum("aec,ecn->ean", columns, shard_piece, preferred_element_type=jnp.float32)
    inside = member & (slot_index >= 0) & (slot_index < piece_rows)
    fetched = jax.vmap(lambda rows_in, picks: jnp.take(rows_in, picks, axis=0))(
        shard_piece, jnp.clip(slot_index, 0, piece_rows - 1)
    )
    kept_rows = jnp.where(inside[:, :, None], fetched, kept_rows)
    product_three, kept_rows = (running, kept_rows)
    chain_rows = kept_rows.reshape(bottom_dev, 3, rows_dev, own_cols)
    off_three = jnp.where(member[:, :, None], -product_three, 0.0).astype(jnp.bfloat16)
    off_three = off_three.reshape(bottom_dev, 3, rows_dev, own_cols)
    full_three = lax.all_gather(off_three, "col", axis=3, tiled=True)
    term_three = jnp.einsum(
        "ekin,ekim->enm", chain_rows, full_three, preferred_element_type=jnp.float32
    )
    summed_three = lax.psum_scatter(
        term_three.astype(jnp.bfloat16), "row", scatter_dimension=2, tiled=True
    ).astype(jnp.float32)
    mask_rows_three = row_index[None, :] < width_three[:, None]
    inverse_three = jnp.where(
        mask_cols_three[:, :, None] & mask_rows_three[:, None, :], bottom_inverse, 0
    ).astype(jnp.float32)
    diag_three = (inverse_three - summed_three).astype(jnp.bfloat16)
    return (second_off, second_diag, off_two[None], diag_two[None], off_three, diag_three)


def solution(mesh):
    in_specs = (
        P(),
        P("leaf", None),
        P("row", None),
        P("leaf", "row", "col"),
        P("leaf", "col", "row"),
        P("leaf", None, "row", "col"),
        P("leaf", "col", "row"),
        P("leaf", "row", "col"),
        P("leaf", "col", "row"),
    )
    out_specs = (
        P("leaf", "row", "col"),
        P("leaf", "col", "row"),
        P("leaf", None, "row", "col"),
        P("leaf", "col", "row"),
        P("leaf", None, "row", "col"),
        P("leaf", "col", "row"),
    )
    return jax.shard_map(local, mesh=mesh, in_specs=in_specs, out_specs=out_specs, check_vma=False)
```

profile of v0, /device:TPU:0, one launch (start us, length us, event | category | flops | bytes accessed | tf_op | source)
XLA Modules:
  0.0 1248.3 jit_solution(15678151634752697169)
XLA Ops:
  7.2 1.3 copy.59
  8.5 1.3 fusion.30
  9.8 0.7 add_compare_fusion
  10.5 0.9 bitcast_select_fusion.1
  11.5 0.7 fusion.26
  12.2 0.7 iota_compare_fusion
  12.8 2.3 and_select_fusion.1
  15.1 44.9 %all-gather.9.cloned.1.call-done = bf16[2048,512]{0,1:T(8,128)(2,1)} async-done(((bf16[512,512]{0,1:T(8,128)(2,1)}), bf16[2048,512]{0,1:T(8,128)(2,1)}) %all-gather.9.cloned.1.call-update) | async-done | bytes 2097168 | tf_op jit(solution)/shard_map/all_gather | solution.py:68
  60.0 3.7 fusion.12
  63.7 20.2 %all-gather.11.cloned.1.call-done = bf16[512,1024]{1,0:T(8,128)(2,1)} async-done(((bf16[512,512]{1,0:T(8,128)(2,1)}), bf16[512,1024]{1,0:T(8,128)(2,1)}) %all-gather.11.cloned.1.call-update) | async-done | bytes 1048592 | tf_op jit(solution)/shard_map/all_gather | solution.py:72
  83.9 2.9 collective-permute-done
  86.8 2.7 maximum_select_fusion
  89.5 1.3 copy-done
  90.8 2.6 convolution_convert_fusion
  93.6 2.0 copy.60
  95.6 0.7 fusion.25
  96.3 41.0 %reduce-scatter.4.cloned.1.call-done = bf16[512,512]{0,1:T(8,128)(2,1)} async-done(((bf16[512,2048]{0,1:T(8,128)(2,1)}), bf16[512,512]{0,1:T(8,128)(2,1)}) %reduce-scatter.4.cloned.1.call-update) | async-done | bytes 524304 | tf_op jit(solution)/shard_map/reduce_scatter | solution.py:82
  137.3 2.5 fusion.34
  140.4 3.0 bitcast_select_fusion
  143.6 1.3 copy.92
  144.9 1.6 maximum_select_fusion.1
  146.5 4.4 all-to-all-start
  151.0 9.4 all-gather.13.cloned.1.call-done
  160.4 3.9 maximum_bitcast_fusion.3
  164.4 75.7 %all-to-all-done = bf16[512,4,512]{2,0,1:T(8,128)(2,1)} async-done(((bf16[512,4,512]{2,0,1:T(8,128)(2,1)}), bf16[512,4,512]{2,0,1:T(8,128)(2,1)}, u32[]{:S(2)}, u32[]{:S(2)}) %all-to-all-start) | async-done | bytes 2097184 | tf_op jit(solution)/shard_map/all_to_all | solution.py:98
  240.1 3.9 copy.81
  244.1 2.5 maximum_select_fusion.2
  246.6 1.4 copy-done.4
  248.0 2.5 maximum_bitcast_fusion.4
  250.5 7.5 pad_maximum_fusion.1
  258.0 76.6 %all-gather.15.cloned.1.call-done = bf16[2,2048,1024]{2,1,0:T(8,128)(2,1)} async-done(((bf16[2,512,1024]{2,1,0:T(8,128)(2,1)}), bf16[2,2048,1024]{2,1,0:T(8,128)(2,1)}) %all-gather.15.cloned.1.call-update) | async-done | bytes 8388624 | tf_op jit(solution)/shard_map/all_gather | solution.py:109
  334.5 14.6 %negate_convert_fusion = bf16[1024,1024]{1,0:T(8,128)(2,1)} fusion(bf16[1024,4096]{1,0:T(8,128)(2,1)} %bitcast.115, bf16[4096,1024]{1,0:T(8,128)(2,1)} %bitcast.128), kind=kOutput, calls=%fused_computation.21 | convolution fusion | flops 8592031744 | bytes 18874368 | tf_op jit(solution)/shard_map/dot_general | solution.py:34
  349.5 55.6 %all-gather.17.cloned.1.call-done = bf16[2,512,2048]{2,1,0:T(8,128)(2,1)} async-done(((bf16[2,512,1024]{2,1,0:T(8,128)(2,1)}), bf16[2,512,2048]{2,1,0:T(8,128)(2,1)}) %all-gather.17.cloned.1.call-update) | async-done | bytes 4194320 | tf_op jit(solution)/shard_map/all_gather | solution.py:112
  405.1 9.4 bitcast_convert_fusion.1
  414.6 1.5 copy.67
  416.6 74.8 %reduce-scatter.6.cloned.1.call-done = bf16[1024,512]{0,1:T(8,128)(2,1)} async-done(((bf16[1024,2048]{0,1:T(8,128)(2,1)}), bf16[1024,512]{0,1:T(8,128)(2,1)}) %reduce-scatter.6.cloned.1.call-update) | async-done | bytes 1048592 | tf_op jit(solution)/shard_map/reduce_scatter | solution.py:114
  491.5 3.1 fusion.36
  496.0 4.4 broadcast_select_fusion
  500.5 11.2 copy.70
  511.8 5.0 all-to-all-start.1
  516.9 0.7 add_select_fusion.2
  517.6 0.6 add_select_fusion.1
  519.0 2.9 slice_bitcast_fusion.1
  522.5 0.6 copy-done.5
  523.1 5.1 maximum_bitcast_fusion
  528.2 191.2 %all-to-all-done.1 = bf16[2,512,2048]{1,0,2:T(2,128)(2,1)} async-done(((bf16[2,512,2048]{1,0,2:T(2,128)(2,1)}), bf16[2,512,2048]{1,0,2:T(2,128)(2,1)}, u32[]{:S(2)}, u32[]{:S(2)}) %all-to-all-start.1) | async-done | bytes 4194336 | tf_op jit(solution)/shard_map/all_to_all | solution.py:123
  719.4 5.1 copy.85
  724.4 4.5 copy.87
  728.9 6.4 maximum_bitcast_fusion.2
  735.3 12.1 pad_maximum_fusion
  747.5 24.7 %copy.72 = bf16[1536,6144]{0,1:T(8,128)(2,1)} copy(bf16[1536,6144]{1,0:T(8,128)(2,1)} %bitcast.107) | data formatting | bytes 37748736 | tf_op jit(solution)/shard_map/reshape | solution.py:133
  772.2 58.3 %gather_fusion = bf16[8192,1536]{1,0:T(8,128)(2,1)} fusion(bf16[1536,6144]{0,1:T(8,128)(2,1)} %copy.72, s32[8192]{0:T(1024)S(1)} %broadcast_clamp_fusion), kind=kCustom, calls=%fused_computation | custom fusion | bytes 50364416 | tf_op jit(solution)/shard_map/jit(_take)/gather | solution.py:158
  830.5 32.1 %copy.73 = bf16[1536,2,4096]{2,0,1:T(8,128)(2,1)} copy(bf16[1536,2,4096]{0,2,1:T(8,128)(2,1)} %bitcast.106) | data formatting | bytes 50331648 | tf_op jit(solution)/shard_map/jit(_take)/gather | solution.py:158
  862.5 18.1 %all-gather.21.cloned.1.call-done = bf16[2,4096,1024]{2,1,0:T(8,128)(2,1)} async-done(((bf16[2,1024,1024]{2,1,0:T(8,128)(2,1)}), bf16[2,4096,1024]{2,1,0:T(8,128)(2,1)}) %all-gather.21.cloned.1.call-update) | async-done | bytes 16777232 | tf_op jit(solution)/shard_map/all_gather | solution.py:155
  880.6 41.7 %select_convert_fusion = bf16[2,1536,1024]{2,1,0:T(8,128)(2,1)} fusion(bf16[2,4096,1024]{2,1,0:T(8,128)(2,1)} %all-gather.21.cloned.1.call-done, bf16[1536,2,4096]{2,0,1:T(8,128)(2,1)} %copy.73, pred[2,4096]{1,0:T(4,128)(4,1)S(1)} %compare_and_fusion, pred[2,1536]{1,0:T(4,128)(4,1)S(1)} %compare_reduce_fusion), kind=kOutput, calls=%fused_computation.7 | convolution fusion | flops 25791823872 | bytes 48245760 | tf_op jit(solution)/shard_map/aec,ecn->ean/dot_general | solution.py:161
  923.3 62.6 %gather_fusion.1 = bf16[3072,1024]{1,0:T(8,128)(2,1)} fusion(bf16[2,4096,1024]{2,1,0:T(8,128)(2,1)} %all-gather.21.cloned.1.call-done, s32[3072]{0:T(1024)S(1)} %reshape.373), kind=kCustom, calls=%fused_computation.1 | custom fusion | bytes 12607488 | tf_op jit(solution)/shard_map/vmap(jit(_take))/gather | solution.py:163
  986.0 8.7 copy.74
  994.6 78.9 %all-gather.23.cloned.1.call-done = bf16[2,3,512,2048]{3,2,1,0:T(8,128)(2,1)} async-done(((bf16[2,3,512,1024]{3,2,1,0:T(8,128)(2,1)}), bf16[2,3,512,2048]{3,2,1,0:T(8,128)(2,1)}) %all-gather.23.cloned.1.call-update) | async-done | bytes 12582928 | tf_op jit(solution)/shard_map/all_gather | solution.py:171
  1073.6 20.0 %bitcast_convert_fusion = bf16[2,1024,2048]{2,1,0:T(8,128)(2,1)} fusion(bf16[2,3,512,2048]{3,2,1,0:T(8,128)(2,1)} %all-gather.23.cloned.1.call-done, bf16[2,3,512,1024]{2,3,1,0:T(8,128)(2,1)} %copy.74, pred[2,3,512]{2,1,0:T(4,128)(4,1)S(1)} %get-tuple-element.40, pred[2,3,512]{2,1,0:T(4,128)(4,1)S(1)} %get-tuple-element.39), kind=kOutput, calls=%fused_computation.6 | convolution fusion | flops 12895387648 | bytes 27269120 | tf_op jit(solution)/shard_map/ekin,ekim->enm/dot_general | solution.py:172
  1093.6 0.6 copy-done.19
  1094.3 2.3 copy.75
  1096.5 1.3 copy.76
  1097.9 140.5 %reduce-scatter.8.cloned.1.call-done = bf16[2,1024,512]{2,1,0:T(8,128)(2,1)} async-done(((bf16[2,1024,2048]{2,1,0:T(8,128)(2,1)}), bf16[2,1024,512]{2,1,0:T(8,128)(2,1)}) %reduce-scatter.8.cloned.1.call-update) | async-done | bytes 2097168 | tf_op jit(solution)/shard_map/reduce_scatter | solution.py:175
  1238.4 3.2 subtract_convert_fusion
  (105 shorter events, 5.9 us)
Async XLA Ops:
  7.2 52.8 %all-gather.9.cloned.1.call-start = ((), (), s32[]{:S(2)}) async-start(), calls=%async_computation.5 | async-start | bytes 2621440 | tf_op jit(solution)/shard_map/all_gather | solution.py:68
  11.4 72.5 %all-gather.11.cloned.1.call-start = ((), (), s32[]{:S(2)}) async-start(), calls=%async_computation.6 | async-start | bytes 1572864 | tf_op jit(solution)/shard_map/all_gather | solution.py:72
  63.7 73.6 %reduce-scatter.4.cloned.1.call-start = ((), (), s32[]{:S(2)}) async-start(), calls=%async_computation.7 | async-start | bytes 2621440 | tf_op jit(solution)/shard_map/reduce_scatter | solution.py:82
  83.9 2.9 collective-permute-start
  83.9 6.9 copy-start.10
  86.8 6.7 copy-start.8
  89.5 1.4 copy-start
  93.5 66.9 %all-gather.13.cloned.1.call-start = ((), (), s32[]{:S(2)}) async-start(), calls=%async_computation.8 | async-start | bytes 1572864 | tf_op jit(solution)/shard_map/all_gather | solution.py:89
  96.3 47.2 %copy-start.7 = (bf16[512,1024]{1,0:T(8,128)(2,1)S(1)}, bf16[512,1024]{1,0:T(8,128)(2,1)}, u32[]{:S(2)}) copy-start(bf16[512,1024]{1,0:T(8,128)(2,1)} %all-gather.11.cloned.1.call-done) | copy-start | bytes 3145732
  139.8 194.7 %all-gather.15.cloned.1.call-start = ((), (), s32[]{:S(2)}) async-start(), calls=%async_computation.9 | async-start | bytes 10485760 | tf_op jit(solution)/shard_map/all_gather | solution.py:109
  146.5 93.6 %all-to-all-start = ((bf16[512,4,512]{2,0,1:T(8,128)(2,1)}), bf16[512,4,512]{2,0,1:T(8,128)(2,1)}, u32[]{:S(2)}, u32[]{:S(2)}) async-start(bf16[512,4,512]{2,0,1:T(8,128)(2,1)} %maximum_select_fusion.1), calls=%async_computation.1 | async-start | bytes 4194304 | tf_op jit(solution)/shard_map/all_to_all | solution.py:98
  151.0 254.1 %all-gather.17.cloned.1.call-start = ((), (), s32[]{:S(2)}) async-start(), calls=%async_computation.10 | async-start | bytes 6291456 | tf_op jit(solution)/shard_map/all_gather | solution.py:112
  160.4 83.6 %collective-permute-start.1 = (bf16[512,1024]{1,0:T(8,128)(2,1)}, bf16[512,1024]{1,0:T(8,128)(2,1)}, u32[]{:S(2)}, u32[]{:S(2)}) collective-permute-start(bf16[512,1024]{1,0:T(8,128)(2,1)} %all-gather.13.cloned.1.call-done), channel_id=1, source_target_pairs={{0,8},{8,0},{16,24},{24,16},{1,9},{9,1},{17,25},{25,17},{2,10},{10... | collective-permute-start | bytes 3145736 | tf_op jit(solution)/shard_map/ppermute | solution.py:17
  164.4 79.7 %copy-start.11 = (bf16[512,1024]{1,0:T(8,128)(2,1)S(1)}, bf16[512,1024]{1,0:T(8,128)(2,1)}, u32[]{:S(2)}) copy-start(bf16[512,1024]{1,0:T(8,128)(2,1)} %all-gather.13.cloned.1.call-done) | copy-start | bytes 3145732
  244.0 3.9 copy-start.2
  246.6 1.4 copy-start.4
  349.2 142.3 %reduce-scatter.6.cloned.1.call-start = ((), (), s32[]{:S(2)}) async-start(), calls=%async_computation.11 | async-start | bytes 5242880 | tf_op jit(solution)/shard_map/reduce_scatter | solution.py:114
  414.5 80.1 %copy-start.24 = (s32[15]{0:T(128)S(1)}, s32[15]{0:T(128)}, u32[]{:S(2)}) copy-start(s32[15]{0:T(128)} %param.9) | copy-start | bytes 184
  414.5 314.4 %all-gather.19.cloned.1.call-start = ((), (), s32[]{:S(2)}) async-start(), calls=%async_computation.12 | async-start | bytes 3145728 | tf_op jit(solution)/shard_map/all_gather | solution.py:122
  494.6 386.1 %all-gather.21.cloned.1.call-start = ((), (), s32[]{:S(2)}) async-start(), calls=%async_computation.13 | async-start | bytes 20971520 | tf_op jit(solution)/shard_map/all_gather | solution.py:155
  494.8 0.5 copy-start.22
  495.4 0.6 copy-start.14
  511.8 6.4 copy-start.20
  511.8 207.6 %all-to-all-start.1 = ((bf16[2,512,2048]{1,0,2:T(2,128)(2,1)}), bf16[2,512,2048]{1,0,2:T(2,128)(2,1)}, u32[]{:S(2)}, u32[]{:S(2)}) async-start(bf16[2,512,2048]{1,0,2:T(2,128)(2,1)} %copy.70), calls=%async_computation.3 | async-start | bytes 8388608 | tf_op jit(solution)/shard_map/all_to_all | solution.py:123
  516.7 556.8 %all-gather.23.cloned.1.call-start = ((), (), s32[]{:S(2)}) async-start(), calls=%async_computation.14 | async-start | bytes 18874368 | tf_op jit(solution)/shard_map/all_gather | solution.py:171
  516.9 0.7 copy-start.18
  518.2 0.6 copy-start.12
  519.0 2.9 copy-start.1
  519.0 3.5 copy-start.3
  519.0 4.1 copy-start.5
  728.9 6.4 slice-start
  728.9 6.4 slice-start.1
  922.3 0.7 copy-start.13
  922.3 0.7 copy-start.21
  922.3 0.8 copy-start.17
  922.3 0.9 copy-start.16
  922.3 316.0 %reduce-scatter.8.cloned.1.call-start = ((), (), s32[]{:S(2)}) async-start(), calls=%async_computation.15 | async-start | bytes 10485760 | tf_op jit(solution)/shard_map/reduce_scatter | solution.py:175
  1093.5 0.7 copy-start.19
  1093.5 0.7 copy-start.23
  1093.5 3.0 copy-start.6
  1093.5 144.8 %copy-start.9 = (bf16[2,1024,512]{2,1,0:T(8,128)(2,1)S(1)}, bf16[2,1024,512]{2,1,0:T(8,128)(2,1)}, u32[]{:S(2)}) copy-start(bf16[2,1024,512]{2,1,0:T(8,128)(2,1)} %param.17) | copy-start | bytes 6291460
  1093.6 144.8 %copy-start.15 = (pred[2,1024]{1,0:T(4,128)(4,1)S(1)}, pred[2,1024]{1,0:T(4,128)(4,1)}, u32[]{:S(2)}) copy-start(pred[2,1024]{1,0:T(4,128)(4,1)} %copy-done.14) | copy-start | bytes 6148
Sparse Core Ops, SparseCore 0:
  11.6 48.3 all-gather.8
  63.8 20.0 all-gather.10
  93.6 43.6 reduce-scatter.3
  139.9 20.4 all-gather.12
  161.9 172.6 all-gather.14
  349.3 55.7 all-gather.16
  414.6 76.7 reduce-scatter.5
  494.7 33.6 all-gather.18
  529.9 350.6 all-gather.20
  922.5 151.0 all-gather.22
  1093.7 144.6 reduce-scatter.7
where the time goes:
time: 1260 us; the launch traced here: 1250 us
  waiting for transfers between devices  830 us (66%)
  local copies, waits for them, and re-layouts  231 us (18%)
  matrix products  91.9 us (7%)
  other arithmetic  71.1 us (6%)
  between operations  14.5 us (1%)
    all_to_all x1, waiting for transfers between devices, local(): lax.all_to_all(full_two, 'row', split_axis=2, concat_axis=1, tiled=True)  191 us
    reduce_scatter x1, waiting for transfers between devices, local(): lax.psum_scatter(term_three.astype(jnp.bfloat16), 'row', scatter_dimensio...  141 us
    gather x2, local copies, waits for them, and re-layouts, local(): jnp.take(flat_three, positions.reshape(-1), axis=1)  90.3 us
    all_gather x1, waiting for transfers between devices, local(): full_three = lax.all_gather(off_three, 'col', axis=3, tiled=True)  78.9 us
    all_gather x1, waiting for transfers between devices, local(): lax.all_gather(panel_two, 'row', axis=1, tiled=True)  76.6 us
    all_to_all x1, waiting for transfers between devices, local(): lax.all_to_all(off_full, 'row', split_axis=1, concat_axis=0, tiled=True)  75.7 us
    reduce_scatter x1, waiting for transfers between devices, local(): lax.psum_scatter(term_two.astype(jnp.bfloat16), 'row', scatter_dimension=...  74.8 us
    gather x3, local copies, waits for them, and re-layouts, local(): jnp.take(rows_in, picks, axis=0)  71.3 us
  transfers between devices with their start and end apart: 15, of which 13 were waited for; matrix products, arithmetic and copies ran while one was open for 22% of the time, Pallas kernels for 0%

commit v1 on v0

--- a/solution.py
+++ b/solution.py
@@ -1,6 +1,8 @@
 import jax
 import jax.numpy as jnp
 from jax import lax
+from jax.experimental import pallas as pl
+from jax.experimental.pallas import tpu as pltpu
 from jax.sharding import PartitionSpec as P
 
 NODES = 15
@@ -34,7 +36,7 @@
     return jnp.dot(picked, stacked, preferred_element_type=jnp.float32)
 
 
-def local(
+def local_general(
     widths,
     bottom_lists,
     root_inverse,
@@ -183,6 +185,202 @@
     return (second_off, second_diag, off_two[None], diag_two[None], off_three, diag_three)
 
 
+def copy_block(picks, blocks_in, blocks_out):
+    blocks_out[...] = blocks_in[...]
+
+
+def pick_columns(matrix, picks, width):
+    rows = matrix.shape[0]
+    count = picks.shape[0]
+    return pl.pallas_call(
+        copy_block,
+        out_shape=jax.ShapeDtypeStruct((rows, count * width), matrix.dtype),
+        grid_spec=pltpu.PrefetchScalarGridSpec(
+            num_scalar_prefetch=1,
+            grid=(count,),
+            in_specs=[pl.BlockSpec((rows, width), lambda j, picks: (0, picks[j]))],
+            out_specs=pl.BlockSpec((rows, width), lambda j, picks: (0, j)),
+        ),
+        cost_estimate=pl.CostEstimate(
+            flops=0, transcendentals=0, bytes_accessed=4 * rows * count * width
+        ),
+        name="pick_columns",
+    )(picks, matrix)
+
+
+def pick_rows(matrix, picks, height):
+    columns = matrix.shape[1]
+    count = picks.shape[0]
+    return pl.pallas_call(
+        copy_block,
+        out_shape=jax.ShapeDtypeStruct((count * height, columns), matrix.dtype),
+        grid_spec=pltpu.PrefetchScalarGridSpec(
+            num_scalar_prefetch=1,
+            grid=(count,),
+            in_specs=[pl.BlockSpec((height, columns), lambda j, picks: (picks[j], 0))],
+            out_specs=pl.BlockSpec((height, columns), lambda j, picks: (j, 0)),
+        ),
+        cost_estimate=pl.CostEstimate(
+            flops=0, transcendentals=0, bytes_accessed=4 * columns * count * height
+        ),
+        name="pick_rows",
+    )(picks, matrix)
+
+
+def beside(mine, other, place, axis):
+    return jnp.where(
+        place == 0,
+        jnp.concatenate([mine, other], axis),
+        jnp.concatenate([other, mine], axis),
+    )
+
+
+def both_columns(block, col_at, axis):
+    other = lax.ppermute(block, "col", [(0, 1), (1, 0)])
+    return beside(block, other, col_at, axis)
+
+
+def product(left, right):
+    return jnp.dot(left, right, preferred_element_type=jnp.float32)
+
+
+def inner(left, right):
+    return lax.dot_general(
+        left, right, (((0,), (0,)), ((), ())), preferred_element_type=jnp.float32
+    )
+
+
+def local_paired(
+    widths,
+    bottom_lists,
+    root_inverse,
+    second_panels,
+    second_inverse,
+    third_panels,
+    third_inverse,
+    bottom_panels,
+    bottom_inverse,
+):
+    group_at = lax.axis_index("leaf")
+    row_at = lax.axis_index("row")
+    col_at = lax.axis_index("col")
+    rows_dev = root_inverse.shape[0]
+    tile_width = root_inverse.shape[1]
+    half_cols = second_panels.shape[2]
+    own_cols = third_panels.shape[3]
+    half_at = group_at % 2
+    row_first = row_at * rows_dev
+    first_own = col_at * own_cols
+    row_index = row_first + jnp.arange(rows_dev)
+    all_index = jnp.arange(tile_width)
+    own_index = first_own + jnp.arange(own_cols)
+
+    root_width = node_width(widths, 0)
+    root_mask = (row_index < root_width)[:, None] & (all_index < root_width)[None, :]
+    root_block = jnp.where(root_mask, root_inverse, 0)
+    shares = lax.axis_size("leaf") * lax.axis_size("col")
+    share_rows = rows_dev // shares
+    share_at = group_at * lax.axis_size("col") + col_at
+    root_share = lax.dynamic_slice_in_dim(root_block, share_at * share_rows, share_rows, 0)
+    root_full = lax.all_gather(root_share, ("row", "leaf", "col"), axis=0, tiled=True)
+
+    panel_quarter = lax.all_gather(second_panels[0], "row", axis=0, tiled=True)
+    panel_half = both_columns(panel_quarter, col_at, 1)
+    panel_one = beside(panel_half, partner(panel_half, "leaf", 0), half_at, 1)
+    inverse_half = both_columns(second_inverse[0], col_at, 0)
+    inverse_one = beside(inverse_half, partner(inverse_half, "leaf", 0), half_at, 0)
+
+    width_one = node_width(widths, 1 + group_at // 2)
+    keep_one = all_index < width_one
+    keep_rows_one = row_index < width_one
+    off_one = jnp.where(keep_one[None, :], -product(root_block, panel_one), 0).astype(jnp.bfloat16)
+    panel_turn = lax.dynamic_slice_in_dim(panel_one, row_first, rows_dev, 1)
+    turn_one = jnp.where(keep_rows_one[None, :], -product(root_full, panel_turn), 0).astype(
+        jnp.bfloat16
+    )
+    mask_one = keep_one[:, None] & keep_rows_one[None, :]
+    diag_one = jnp.where(
+        mask_one, inverse_one.astype(jnp.float32) - inner(panel_one, turn_one), 0
+    ).astype(jnp.bfloat16)
+    quarter_first = half_at * (tile_width // 2) + col_at * half_cols
+    second_off = lax.dynamic_slice_in_dim(off_one, quarter_first, half_cols, 1)[None]
+    second_diag = lax.dynamic_slice_in_dim(diag_one, quarter_first, half_cols, 0)[None]
+    upper_two = jnp.concatenate([root_block, off_one], 1)
+    lower_two = jnp.concatenate([turn_one, diag_one], 0).T
+    chain_two = jnp.concatenate([upper_two, lower_two], 0)
+
+    panel_two = lax.all_gather(third_panels[0], "row", axis=1, tiled=True)
+    panel_two = panel_two.reshape(2 * tile_width, own_cols)
+    width_two = node_width(widths, 3 + group_at)
+    keep_two = own_index < width_two
+    keep_rows_two = row_index < width_two
+    off_two = jnp.where(keep_two[None, :], -product(chain_two, panel_two), 0).astype(jnp.bfloat16)
+    off_two = off_two.reshape(2, rows_dev, own_cols)
+    full_two = both_columns(off_two, col_at, 2)
+    turn_share = lax.dynamic_index_in_dim(full_two, col_at, 0, keepdims=False)
+    turn_share = lax.all_to_all(turn_share, "row", split_axis=1, concat_axis=0, tiled=True)
+    turn_two = both_columns(turn_share, col_at, 0)
+    mask_two = keep_two[:, None] & keep_rows_two[None, :]
+    diag_two = jnp.where(
+        mask_two, third_inverse[0].astype(jnp.float32) - inner(panel_two, turn_two), 0
+    ).astype(jnp.bfloat16)
+    diag_full = both_columns(diag_two, col_at, 0)
+    chain_three = jnp.concatenate(
+        [
+            jnp.concatenate([chain_two, full_two.reshape(2 * rows_dev, tile_width)], 1),
+            jnp.concatenate([turn_two, diag_full], 0).T,
+        ],
+        0,
+    )
+
+    bottom_dev = bottom_panels.shape[0]
+    list_len = bottom_lists.shape[1]
+    block_rows = 2 * tile_width // list_len
+    dev_blocks = rows_dev // block_rows
+    chain_blocks = (
+        jnp.arange(3)[:, None] * (tile_width // block_rows)
+        + row_at * dev_blocks
+        + jnp.arange(dev_blocks)[None, :]
+    ).reshape(-1)
+    offs = []
+    diags = []
+    for at in range(bottom_dev):
+        listed = bottom_lists[at]
+        matches = listed[:, None] == chain_blocks[None, :]
+        member = jnp.any(matches, axis=0)
+        slots = jnp.sum(jnp.where(matches, jnp.arange(list_len)[:, None], 0), axis=0)
+        member_rows = jnp.repeat(member, block_rows)
+        width_three = node_width(widths, NODES - BOTTOM + bottom_dev * group_at + at)
+        keep_three = own_index < width_three
+        keep_rows_three = row_index < width_three
+        panel_three = lax.all_gather(bottom_panels[at], "row", axis=0, tiled=True)
+        chain_listed = pick_columns(chain_three, listed, block_rows)
+        off_three = jnp.where(
+            member_rows[:, None] & keep_three[None, :], -product(chain_listed, panel_three), 0
+        ).astype(jnp.bfloat16)
+        full_three = both_columns(off_three, col_at, 1)
+        kept_rows = pick_rows(panel_three, slots, block_rows)
+        term_three = inner(kept_rows, full_three).astype(jnp.bfloat16)
+        summed_three = lax.psum_scatter(term_three, "row", scatter_dimension=1, tiled=True)
+        mask_three = keep_three[:, None] & keep_rows_three[None, :]
+        diags.append(
+            jnp.where(
+                mask_three,
+                bottom_inverse[at].astype(jnp.float32) - summed_three.astype(jnp.float32),
+                0,
+            ).astype(jnp.bfloat16)
+        )
+        offs.append(off_three.reshape(3, rows_dev, own_cols))
+    return (
+        second_off,
+        second_diag,
+        off_two[None],
+        diag_two[None],
+        jnp.stack(offs),
+        jnp.stack(diags),
+    )
+
+
 def solution(mesh):
     in_specs = (
         P(),
@@ -203,4 +401,5 @@
         P("leaf", None, "row", "col"),
         P("leaf", "col", "row"),
     )
-    return jax.shard_map(local, mesh=mesh, in_specs=in_specs, out_specs=out_specs, check_vma=False)
+    body = local_paired if mesh.shape["col"] == 2 else local_general
+    return jax.shard_map(body, mesh=mesh, in_specs=in_specs, out_specs=out_specs, check_vma=False)

time: 1260 us -> 939 us (0.75)
  waiting for transfers between devices: 830 us -> 500 us
  local copies, waits for them, and re-layouts: 231 us -> 36.4 us
  blocking collectives: 0 us -> 107 us
  Pallas kernels: 0 us -> 61 us
  matrix products: 91.9 us -> 120 us
    ppermute x0 -> x7, waiting for transfers between devices: none -> 280 us  [both_columns(): other = lax.ppermute(block, 'col', [(0, 1), (1, 0)])]
    all_to_all x2 -> x0, waiting for transfers between devices: 267 us -> none  [the longest x1 191 us: local(): lax.all_to_all(full_two, 'row', split_axis=2, concat_axis=1, tiled=True)]
    reduce_scatter x3 -> x2, waiting for transfers between devices: 256 us -> 55.4 us  [local_paired(): lax.psum_scatter(term_three, 'row', scatter_dimension=1, tiled=True)]
    gather x5 -> x0, local copies, waits for them, and re-layouts: 162 us -> none  [the longest x2 90.3 us: local(): jnp.take(flat_three, positions.reshape(-1), axis=1)]
    all_gather x8 -> x5, waiting for transfers between devices: 304 us -> 163 us  [the longest x1 120 us: local_paired(): panel_two = lax.all_gather(third_panels[0], 'row', axis=1, tiled=True)]
    all_to_all x0 -> x1, blocking collectives: none -> 107 us  [local_paired(): lax.all_to_all(turn_share, 'row', split_axis=1, concat_axis=0, tiled=True)]
    pallas_call x0 -> x4, Pallas kernels: none -> 61 us  [the longest x2 43.8 us: pick_columns(): pl.pallas_call(copy_block, out_shape=jax.ShapeDtypeStruct((rows, count *...]
    dot_general x6 -> x9, matrix products: 91.9 us -> 120 us  [the longest x5 74.7 us: product(): return jnp.dot(left, right, preferred_element_type=jnp.float32)]
  transfers between devices with their start and end apart: 15 -> 16, of which waited for: 13 -> 10; matrix products, arithmetic and copies ran while one was open for 22% -> 25% of each run, Pallas kernels for 0% -> 7%
where the time goes in v1:
time: 939 us; the launch traced here: 934 us
  waiting for transfers between devices  500 us (53%)
  matrix products  120 us (13%)
  blocking collectives  107 us (11%)
  other arithmetic  83.6 us (9%)
  Pallas kernels  61 us (6%)
  local copies, waits for them, and re-layouts  36.4 us (4%)
  between operations  14.8 us (2%)
  starting transfers between devices  10.8 us (1%)
    ppermute x7, waiting for transfers between devices, both_columns(): other = lax.ppermute(block, 'col', [(0, 1), (1, 0)])  280 us
    all_gather x1, waiting for transfers between devices, local_paired(): panel_two = lax.all_gather(third_panels[0], 'row', axis=1, tiled=True)  120 us
    all_to_all x1, blocking collectives, local_paired(): lax.all_to_all(turn_share, 'row', split_axis=1, concat_axis=0, tiled=True)  107 us
    dot_general x5, matrix products, product(): return jnp.dot(left, right, preferred_element_type=jnp.float32)  74.7 us
    reduce_scatter x2, waiting for transfers between devices, local_paired(): lax.psum_scatter(term_three, 'row', scatter_dimension=1, tiled=True)  55.4 us
    dot_general x4, matrix products, inner(): lax.dot_general(left, right, (((0,), (0,)), ((), ())), preferred_element_...  45.5 us
    pallas_call x2, Pallas kernels, pick_columns(): pl.pallas_call(copy_block, out_shape=jax.ShapeDtypeStruct((rows, count *...  43.8 us
    all_gather x1, waiting for transfers between devices, local_paired(): panel_quarter = lax.all_gather(second_panels[0], 'row', axis=0, tiled=True)  43.4 us
  transfers between devices with their start and end apart: 16, of which 10 were waited for; matrix products, arithmetic and copies ran while one was open for 25% of the time, Pallas kernels for 7%

profile of v1, /device:TPU:0, one launch (start us, length us, event | category | flops | bytes accessed | tf_op | source)
XLA Modules:
  0.0 933.7 jit_solution(7363321690123298934)
XLA Ops:
  7.2 0.7 all-gather.12.cloned.1.call-update
  8.0 1.4 fusion.50
  10.7 2.3 and_select_fusion
  13.0 0.7 constant_dynamic-slice_fusion.1
  14.5 43.4 %all-gather.12.cloned.1.call-done = bf16[1,2048,512]{2,1,0:T(8,128)(2,1)} async-done(((bf16[1,512,512]{2,1,0:T(8,128)(2,1)}), bf16[1,2048,512]{2,1,0:T(8,128)(2,1)}) %all-gather.12.cloned.1.call-update) | async-done | bytes 2097168 | tf_op jit(solution)/shard_map/all_gather | solution.py:287
  58.0 1.5 collective-permute-start
  59.4 51.7 %collective-permute-done = bf16[2048,512]{1,0:T(8,128)(2,1)} collective-permute-done((bf16[2048,512]{1,0:T(8,128)(2,1)}, bf16[2048,512]{1,0:T(8,128)(2,1)}, u32[]{:S(2)}, u32[]{:S(2)}) %collective-permute-start) | collective-permute-done | bytes 2097184 | tf_op jit(solution)/shard_map/ppermute | solution.py:239
  111.1 6.5 maximum_select_fusion.5
  117.8 1.5 collective-permute-start.2
  119.4 4.7 fusion.57
  126.3 13.1 %collective-permute-done.2 = bf16[512,512]{0,1:T(8,128)(2,1)S(1)} collective-permute-done((bf16[512,512]{0,1:T(8,128)(2,1)S(1)}, bf16[512,512]{0,1:T(8,128)(2,1)S(1)}, u32[]{:S(2)}, u32[]{:S(2)}) %collective-permute-start.2) | collective-permute-done | bytes 524320 | tf_op jit(solution)/shard_map/ppermute | solution.py:239
  139.4 1.3 maximum_select_fusion.14
  140.7 9.4 %maximum_select_fusion = bf16[2048,2048]{1,0:T(8,128)(2,1)S(1)} fusion(bf16[2048,1024]{1,0:T(8,128)(2,1)} %collective-permute-done.1, bf16[2048,1024]{1,0:T(8,128)(2,1)} %maximum_select_fusion.5, pred[]{:T(512)S(6)} %eq.73), kind=kLoop, calls=%fused_computation.1 | loop fusion | flops 37748736 | bytes 16777216 | tf_op jit(solution)/shard_map/jit(_where)/select_n | solution.py:231
  150.1 3.2 copy-done.2
  153.3 5.8 select_convert_fusion.5
  159.1 9.5 %select_convert_fusion.4 = bf16[2048,512]{0,1:T(8,128)(2,1)S(1)} fusion(bf16[2048,2048]{1,0:T(8,128)(2,1)} %all-gather.10.cloned.1.call-done, bf16[2048,2048]{1,0:T(8,128)(2,1)} %copy-done.2, s32[]{:T(128)S(6)} %select_n.172, pred[512]{0:T(512)(128)(4,1)S(1)} %fusion.44), kind=kOutput, calls=%fused_computation.38 | convolution fusion | flops 4298113024 | bytes 12583428 | tf_op jit(solution)/shard_map/dot_general | solution.py:244
  168.6 6.9 select_convert_fusion.3
  175.5 1.3 copy-done.4
  176.8 2.3 maximum_bitcast_fusion.1
  179.1 119.9 %all-gather.14.cloned.1.call-done = bf16[1,2,2048,1024]{3,2,1,0:T(8,128)(2,1)} async-done(((bf16[1,2,512,1024]{3,2,1,0:T(8,128)(2,1)}), bf16[1,2,2048,1024]{3,2,1,0:T(8,128)(2,1)}) %all-gather.14.cloned.1.call-update) | async-done | bytes 8388624 | tf_op jit(solution)/shard_map/all_gather | solution.py:312
  299.0 20.6 %select_convert_fusion.2 = bf16[1024,1024]{1,0:T(8,128)(2,1)} fusion(bf16[4096,1024]{1,0:T(8,128)(2,1)} %bitcast.74, bf16[512,4096]{1,0:T(8,128)(2,1)} %maximum_bitcast_fusion.1, bf16[512,2048]{1,0:T(8,128)(2,1)} %select_convert_fusion.5, bf16[512,2048]{1,0:T(8,128)(2,1)S(1)} %and_select_fusion, pred[1024]{0:T(1024)(128)(4,1)S(1)} %fusion.40), kind=kOutput, calls=%fused_computation.36 | convolution fusion | flops 8618246144 | bytes 18875392 | tf_op jit(solution)/shard_map/dot_general | solution.py:244
  319.6 3.9 copy.47
  323.5 1.5 collective-permute-start.4
  325.0 46.4 %collective-permute-done.4 = bf16[2,512,1024]{1,2,0:T(8,128)(2,1)} collective-permute-done((bf16[2,512,1024]{1,2,0:T(8,128)(2,1)}, bf16[2,512,1024]{1,2,0:T(8,128)(2,1)}, u32[]{:S(2)}, u32[]{:S(2)}) %collective-permute-start.4) | collective-permute-done | bytes 2097184 | tf_op jit(solution)/shard_map/ppermute | solution.py:239
  371.3 2.9 fusion.25
  374.2 107.0 %all_to_all.19 = bf16[512,4,512]{0,2,1:T(8,128)(2,1)S(1)} all-to-all(bf16[512,4,512]{0,2,1:T(8,128)(2,1)S(1)} %bitcast.63), channel_id=1, replica_groups=mesh['leaf'=4,'row'=4,'col'=2] {'row'}, dimensions={1} | all-to-all | bytes 4194304 | tf_op jit(solution)/shard_map/all_to_all | solution.py:321
  481.2 1.6 copy.63
  482.9 1.5 collective-permute-start.5
  484.4 1.7 copy.45
  486.9 43.3 %collective-permute-done.5 = bf16[2048,512]{0,1:T(8,128)(2,1)} collective-permute-done((bf16[2048,512]{0,1:T(8,128)(2,1)}, bf16[2048,512]{0,1:T(8,128)(2,1)}, u32[]{:S(2)}, u32[]{:S(2)}) %collective-permute-start.5) | collective-permute-done | bytes 2097184 | tf_op jit(solution)/shard_map/ppermute | solution.py:239
  530.3 5.2 maximum_select_fusion.6
  535.5 9.6 %fusion.32 = bf16[1024,512]{0,1:T(8,128)(2,1)S(1)} fusion(bf16[4096,512]{0,1:T(8,128)(2,1)S(1)} %maximum_select_fusion.6, bf16[4096,1024]{1,0:T(8,128)(2,1)} %bitcast.75, bf16[1,1024,512]{1,2,0:T(8,128)(2,1)S(1)} %copy-done.6, pred[1024]{0:T(1024)(128)(4,1)S(1)} %fusion.40, pred[512]{0:T(512)(128)(4,1)S(1)} %fusion.43), kind=kOutput, calls=%fused_computation.57 | convolution fusion | flops 4297588736 | bytes 14681600 | tf_op jit(solution)/shard_map/dot_general | solution.py:248
  545.1 1.5 collective-permute-start.6
  547.5 4.0 copy.50
  551.5 6.7 maximum_select_fusion.7
  558.2 10.8 %collective-permute-done.6 = bf16[1024,512]{0,1:T(8,128)(2,1)} collective-permute-done((bf16[1024,512]{0,1:T(8,128)(2,1)S(1)}, bf16[1024,512]{0,1:T(8,128)(2,1)}, u32[]{:S(2)}, u32[]{:S(2)}) %collective-permute-start.6) | collective-permute-done | bytes 1048608 | tf_op jit(solution)/shard_map/ppermute | solution.py:239
  569.0 2.3 maximum_select_fusion.13
  571.3 3.5 maximum_bitcast_fusion
  574.8 22.8 %pad_maximum_fusion.blocks_in = bf16[1536,6144]{1,0:T(8,128)(2,1)} fusion(bf16[512,6144]{1,0:T(8,128)(2,1)} %maximum_bitcast_fusion, bf16[1024,2048]{1,0:T(8,128)(2,1)} %maximum_select_fusion.7, bf16[512,4096]{1,0:T(8,128)(2,1)} %maximum_bitcast_fusion.1, bf16[512,2048]{1,0:T(8,128)(2,1)} %select_convert_fusion.5, bf16[512,2048]{1,0:T(8,128)(2,1)S(1)} %and_select_fusion), kind=kLoop, calls=%fused_computation | loop fusion | flops 94371840 | bytes 37748736 | tf_op jit(solution)/shard_map/concatenate | solution.py:328
  597.5 21.7 %pick_columns.3 = bf16[1536,4096]{1,0:T(8,128)(2,1)} custom-call(s32[32]{0:T(128)} %copy-done.9, bf16[1536,6144]{1,0:T(8,128)(2,1)} %pad_maximum_fusion.blocks_in), custom_call_target="tpu_custom_call" | custom-call | bytes 25165824 | tf_op jit(solution)/shard_map/pick_columns/pallas_call | solution.py:195
  619.3 19.5 %select_convert_fusion = bf16[1536,1024]{1,0:T(8,128)(2,1)} fusion(bf16[1536,4096]{1,0:T(8,128)(2,1)} %pick_columns.3, pred[1024]{0:T(1024)(128)(4,1)S(1)} %fusion.38, pred[1536]{0:T(1024)(128)(4,1)S(1)} %broadcast_bitcast_fusion, bf16[1,4096,1024]{2,1,0:T(8,128)(2,1)} %all-gather.18.cloned.1.call-done), kind=kOutput, calls=%fused_computation.24 | convolution fusion | flops 12891193344 | bytes 24119808 | tf_op jit(solution)/shard_map/dot_general | solution.py:244
  638.7 1.4 collective-permute-start.8
  640.1 0.7 fusion.36
  640.8 8.6 pick_rows.3
  649.4 57.4 %collective-permute-done.8 = bf16[1536,1024]{1,0:T(8,128)(2,1)} collective-permute-done((bf16[1536,1024]{1,0:T(8,128)(2,1)}, bf16[1536,1024]{1,0:T(8,128)(2,1)}, u32[]{:S(2)}, u32[]{:S(2)}) %collective-permute-start.8) | collective-permute-done | bytes 3145760 | tf_op jit(solution)/shard_map/ppermute | solution.py:239
  706.8 14.4 %fusion.20 = bf16[1024,2048]{0,1:T(8,128)(2,1)} fusion(bf16[1536,1024]{1,0:T(8,128)(2,1)} %pick_rows.3, bf16[1536,1024]{1,0:T(8,128)(2,1)} %collective-permute-done.8, bf16[1536,1024]{1,0:T(8,128)(2,1)} %select_convert_fusion, pred[]{:T(512)S(6)} %eq.74), kind=kOutput, calls=%fused_computation.41 | convolution fusion | flops 6472859648 | bytes 13631489 | tf_op jit(solution)/shard_map/dot_general | solution.py:248
  722.1 22.1 %pick_columns.2 = bf16[1536,4096]{1,0:T(8,128)(2,1)} custom-call(s32[32]{0:T(128)} %copy-done.8, bf16[1536,6144]{1,0:T(8,128)(2,1)} %pad_maximum_fusion.blocks_in), custom_call_target="tpu_custom_call" | custom-call | bytes 25165824 | tf_op jit(solution)/shard_map/pick_columns/pallas_call | solution.py:195
  744.1 19.4 %select_convert_fusion.1 = bf16[1536,1024]{1,0:T(8,128)(2,1)} fusion(bf16[1536,4096]{1,0:T(8,128)(2,1)} %pick_columns.2, pred[1024]{0:T(1024)(128)(4,1)S(1)} %fusion.39, pred[1536]{0:T(1024)(128)(4,1)S(1)} %broadcast_bitcast_fusion.1, bf16[1,4096,1024]{2,1,0:T(8,128)(2,1)} %all-gather.16.cloned.1.call-done), kind=kOutput, calls=%fused_computation.25 | convolution fusion | flops 12891193344 | bytes 24119808 | tf_op jit(solution)/shard_map/dot_general | solution.py:244
  763.5 1.4 collective-permute-start.7
  765.0 8.6 pick_rows.2
  773.6 57.2 %collective-permute-done.7 = bf16[1536,1024]{1,0:T(8,128)(2,1)} collective-permute-done((bf16[1536,1024]{1,0:T(8,128)(2,1)}, bf16[1536,1024]{1,0:T(8,128)(2,1)}, u32[]{:S(2)}, u32[]{:S(2)}) %collective-permute-start.7) | collective-permute-done | bytes 3145760 | tf_op jit(solution)/shard_map/ppermute | solution.py:239
  830.7 14.6 %fusion.21 = bf16[1024,2048]{0,1:T(8,128)(2,1)} fusion(bf16[1536,1024]{1,0:T(8,128)(2,1)} %pick_rows.2, bf16[1536,1024]{1,0:T(8,128)(2,1)} %collective-permute-done.7, bf16[1536,1024]{1,0:T(8,128)(2,1)} %select_convert_fusion.1, pred[]{:T(512)S(6)} %eq.74), kind=kOutput, calls=%fused_computation.42 | convolution fusion | flops 6472859648 | bytes 13631489 | tf_op jit(solution)/shard_map/dot_general | solution.py:248
  845.4 2.6 fusion.58
  848.6 1.5 copy.61
  850.1 1.3 fusion.41
  851.3 2.0 dynamic-slice_bitcast_fusion
  853.3 1.9 constant_dynamic-slice_fusion
  855.2 2.0 copy.44
  857.3 1.6 copy.55
  858.8 6.2 pad_maximum_fusion.1
  865.0 1.7 fusion.35
  866.7 55.4 %reduce-scatter.3.cloned.1.call-done = bf16[1024,512]{0,1:T(8,128)(2,1)} async-done(((bf16[1024,2048]{0,1:T(8,128)(2,1)}), bf16[1024,512]{0,1:T(8,128)(2,1)}) %reduce-scatter.3.cloned.1.call-update) | async-done | bytes 1048592 | tf_op jit(solution)/shard_map/reduce_scatter | solution.py:364
  922.1 1.7 fusion.34
  924.0 2.6 copy.56
  (61 shorter events, 7.9 us)
Async XLA Ops:
  7.2 50.8 %all-gather.12.cloned.1.call-start = ((), (), s32[]{:S(2)}) async-start(), calls=%async_computation.6 | async-start | bytes 2621440 | tf_op jit(solution)/shard_map/all_gather | solution.py:287
  7.9 151.2 %all-gather.10.cloned.1.call-start = ((), (), s32[]{:S(2)}) async-start(), calls=%async_computation.3 | async-start | bytes 8650752 | tf_op jit(solution)/shard_map/all_gather | solution.py:285
  13.7 285.2 %all-gather.14.cloned.1.call-start = ((), (), s32[]{:S(2)}) async-start(), calls=%async_computation.7 | async-start | bytes 10485760 | tf_op jit(solution)/shard_map/all_gather | solution.py:312
  14.5 604.8 %all-gather.18.cloned.1.call-start = ((), (), s32[]{:S(2)}) async-start(), calls=%async_computation.9 | async-start | bytes 10485760 | tf_op jit(solution)/shard_map/all_gather | solution.py:356
  58.0 53.2 %collective-permute-start = (bf16[2048,512]{1,0:T(8,128)(2,1)}, bf16[2048,512]{1,0:T(8,128)(2,1)}, u32[]{:S(2)}, u32[]{:S(2)}) collective-permute-start(bf16[2048,512]{1,0:T(8,128)(2,1)} %bitcast.71), channel_id=1, source_target_pairs={{0,1},{1,0},{2,3},{3,2},{4,5},{5,4},{6,7},{7,6},{8,9},{9,8},{10,11... | collective-permute-start | bytes 6291464 | tf_op jit(solution)/shard_map/ppermute | solution.py:239
  59.4 58.2 %copy-start.7 = (bf16[1,512,512]{2,1,0:T(8,128)(2,1)S(1)}, bf16[1,512,512]{2,1,0:T(8,128)(2,1)}, u32[]{:S(2)}) copy-start(bf16[1,512,512]{2,1,0:T(8,128)(2,1)} %param.13) | copy-start | bytes 1572868
  117.6 23.1 %collective-permute-start.1 = (bf16[2048,1024]{1,0:T(8,128)(2,1)}, bf16[2048,1024]{1,0:T(8,128)(2,1)}, u32[]{:S(2)}, u32[]{:S(2)}) collective-permute-start(bf16[2048,1024]{1,0:T(8,128)(2,1)} %maximum_select_fusion.5), channel_id=1, source_target_pairs={{0,8},{8,0},{16,24},{24,16},{1,9},{9,1},{17,25},{25,17},{2,10},{10... | collective-permute-start | bytes 12582920 | tf_op jit(solution)/shard_map/ppermute | solution.py:19
  117.8 21.6 %collective-permute-start.2 = (bf16[512,512]{0,1:T(8,128)(2,1)S(1)}, bf16[512,512]{0,1:T(8,128)(2,1)S(1)}, u32[]{:S(2)}, u32[]{:S(2)}) collective-permute-start(bf16[512,512]{0,1:T(8,128)(2,1)S(1)} %bitcast.69), channel_id=1, source_target_pairs={{0,1},{1,0},{2,3},{3,2},{4,5},{5,4},{6,7},{7,6},{8,9},{9,8},{10,11... | collective-permute-start | bytes 1572872 | tf_op jit(solution)/shard_map/ppermute | solution.py:239
  124.1 620.0 %all-gather.16.cloned.1.call-start = ((), (), s32[]{:S(2)}) async-start(), calls=%async_computation.8 | async-start | bytes 10485760 | tf_op jit(solution)/shard_map/all_gather | solution.py:356
  140.7 27.9 %collective-permute-start.3 = (bf16[1024,512]{0,1:T(8,128)(2,1)}, bf16[1024,512]{0,1:T(8,128)(2,1)S(1)}, u32[]{:S(2)}, u32[]{:S(2)}) collective-permute-start(bf16[1024,512]{0,1:T(8,128)(2,1)} %maximum_select_fusion.14), channel_id=1, source_target_pairs={{0,8},{8,0},{16,24},{24,16},{1,9},{9,1},{17,25},{25,17},{2,10},{10... | collective-permute-start | bytes 3145736 | tf_op jit(solution)/shard_map/ppermute | solution.py:19
  150.1 3.2 copy-start.2
  159.1 9.5 %copy-start.3 = (bf16[2048,2048]{1,0:T(8,128)(2,1)S(1)}, bf16[2048,2048]{1,0:T(8,128)(2,1)}, u32[]{:S(2)}) copy-start(bf16[2048,2048]{1,0:T(8,128)(2,1)} %copy-done.2) | copy-start | bytes 25165828
  175.5 1.3 copy-start.4
  323.5 47.8 %collective-permute-start.4 = (bf16[2,512,1024]{1,2,0:T(8,128)(2,1)}, bf16[2,512,1024]{1,2,0:T(8,128)(2,1)}, u32[]{:S(2)}, u32[]{:S(2)}) collective-permute-start(bf16[2,512,1024]{1,2,0:T(8,128)(2,1)} %copy.47), channel_id=1, source_target_pairs={{0,1},{1,0},{2,3},{3,2},{4,5},{5,4},{6,7},{7,6},{8,9},{9,8},{10,11... | collective-permute-start | bytes 6291464 | tf_op jit(solution)/shard_map/ppermute | solution.py:239
  481.2 3.2 copy-start.5
  482.9 47.4 %collective-permute-start.5 = (bf16[2048,512]{0,1:T(8,128)(2,1)}, bf16[2048,512]{0,1:T(8,128)(2,1)}, u32[]{:S(2)}, u32[]{:S(2)}) collective-permute-start(bf16[2048,512]{0,1:T(8,128)(2,1)} %bitcast.31), channel_id=1, source_target_pairs={{0,1},{1,0},{2,3},{3,2},{4,5},{5,4},{6,7},{7,6},{8,9},{9,8},{10,11... | collective-permute-start | bytes 6291464 | tf_op jit(solution)/shard_map/ppermute | solution.py:239
  484.3 380.7 %reduce-scatter.5.cloned.1.call-start = ((), (), s32[]{:S(2)}) async-start(), calls=%async_computation.5 | async-start | bytes 5242880 | tf_op jit(solution)/shard_map/reduce_scatter | solution.py:364
  486.9 48.5 %copy-start.6 = (bf16[1,1024,512]{1,2,0:T(8,128)(2,1)S(1)}, bf16[1,1024,512]{1,2,0:T(8,128)(2,1)}, u32[]{:S(2)}) copy-start(bf16[1,1024,512]{1,2,0:T(8,128)(2,1)} %copy.45) | copy-start | bytes 3145732
  535.4 9.6 %copy-start = (bf16[4096,512]{0,1:T(8,128)(2,1)}, bf16[4096,512]{0,1:T(8,128)(2,1)S(1)}, u32[]{:S(2)}) copy-start(bf16[4096,512]{0,1:T(8,128)(2,1)S(1)} %maximum_select_fusion.6) | copy-start | bytes 12582916
  535.4 11.8 %copy-start.11 = (s32[2,32]{1,0:T(2,128)S(1)}, s32[2,32]{1,0:T(2,128)}, u32[]{:S(2)}) copy-start(s32[2,32]{1,0:T(2,128)} %param.10) | copy-start | bytes 772
  545.1 23.9 %collective-permute-start.6 = (bf16[1024,512]{0,1:T(8,128)(2,1)S(1)}, bf16[1024,512]{0,1:T(8,128)(2,1)}, u32[]{:S(2)}, u32[]{:S(2)}) collective-permute-start(bf16[1024,512]{0,1:T(8,128)(2,1)S(1)} %fusion.32), channel_id=1, source_target_pairs={{0,1},{1,0},{2,3},{3,2},{4,5},{5,4},{6,7},{7,6},{8,9},{9,8},{10,11... | collective-permute-start | bytes 3145736 | tf_op jit(solution)/shard_map/ppermute | solution.py:239
  547.2 10.9 %copy-start.9 = (s32[32]{0:T(128)}, s32[32]{0:T(128)S(1)}, u32[]{:S(2)}) copy-start(s32[32]{0:T(128)S(1)} %get-tuple-element.38.picks) | copy-start | bytes 388
  547.2 92.9 %copy-start.8 = (s32[32]{0:T(128)}, s32[32]{0:T(128)S(1)}, u32[]{:S(2)}) copy-start(s32[32]{0:T(128)S(1)} %get-tuple-element.37.picks) | copy-start | bytes 388
  558.2 13.2 %copy-start.1 = (bf16[4096,512]{0,1:T(8,128)(2,1)S(1)}, bf16[4096,512]{0,1:T(8,128)(2,1)}, u32[]{:S(2)}) copy-start(bf16[4096,512]{0,1:T(8,128)(2,1)} %copy-done) | copy-start | bytes 12582916
  619.2 20.9 %copy-start.10 = (s32[32]{0:T(128)S(1)}, s32[32]{0:T(128)}, u32[]{:S(2)}) copy-start(s32[32]{0:T(128)} %copy-done.9) | copy-start | bytes 388
  638.7 68.1 %collective-permute-start.8 = (bf16[1536,1024]{1,0:T(8,128)(2,1)}, bf16[1536,1024]{1,0:T(8,128)(2,1)}, u32[]{:S(2)}, u32[]{:S(2)}) collective-permute-start(bf16[1536,1024]{1,0:T(8,128)(2,1)} %select_convert_fusion), channel_id=1, source_target_pairs={{0,1},{1,0},{2,3},{3,2},{4,5},{5,4},{6,7},{7,6},{8,9},{9,8},{10,11... | collective-permute-start | bytes 9437192 | tf_op jit(solution)/shard_map/ppermute | solution.py:239
  721.3 200.8 %reduce-scatter.3.cloned.1.call-start = ((), (), s32[]{:S(2)}) async-start(), calls=%async_computation.4 | async-start | bytes 5242880 | tf_op jit(solution)/shard_map/reduce_scatter | solution.py:364
  763.5 67.2 %collective-permute-start.7 = (bf16[1536,1024]{1,0:T(8,128)(2,1)}, bf16[1536,1024]{1,0:T(8,128)(2,1)}, u32[]{:S(2)}, u32[]{:S(2)}) collective-permute-start(bf16[1536,1024]{1,0:T(8,128)(2,1)} %select_convert_fusion.1), channel_id=1, source_target_pairs={{0,1},{1,0},{2,3},{3,2},{4,5},{5,4},{6,7},{7,6},{8,9},{9,8},{10,11... | collective-permute-start | bytes 9437192 | tf_op jit(solution)/shard_map/ppermute | solution.py:239
Sparse Core Ops, SparseCore 0:
  9.5 48.3 all-gather.11
  61.6 86.6 all-gather.9
  149.9 149.0 all-gather.13
  300.4 192.5 all-gather.17
  494.4 147.7 all-gather.15
  721.4 76.2 reduce-scatter.4
  845.5 76.5 reduce-scatter.2

commit v2 on v1

--- a/solution.py
+++ b/solution.py
@@ -235,9 +235,29 @@
     )
 
 
+def swap_columns(block):
+    return lax.ppermute(block, "col", [(0, 1), (1, 0)])
+
+
 def both_columns(block, col_at, axis):
-    other = lax.ppermute(block, "col", [(0, 1), (1, 0)])
-    return beside(block, other, col_at, axis)
+    return beside(block, swap_columns(block), col_at, axis)
+
+
+def row_route(apart):
+    return [(at, at ^ apart) for at in range(lax.axis_size("row"))]
+
+
+def row_exchange(block, row_at):
+    count = lax.axis_size("row")
+    width = block.shape[1] // count
+    own = lax.dynamic_slice_in_dim(block, row_at * width, width, 1)
+    turned = jnp.zeros((count,) + own.shape, own.dtype)
+    turned = lax.dynamic_update_index_in_dim(turned, own, row_at, 0)
+    for apart in range(1, count):
+        sent = lax.dynamic_slice_in_dim(block, (row_at ^ apart) * width, width, 1)
+        came = lax.ppermute(sent, "row", row_route(apart))
+        turned = lax.dynamic_update_index_in_dim(turned, came, row_at ^ apart, 0)
+    return turned
 
 
 def product(left, right):
@@ -278,14 +298,16 @@
     root_width = node_width(widths, 0)
     root_mask = (row_index < root_width)[:, None] & (all_index < root_width)[None, :]
     root_block = jnp.where(root_mask, root_inverse, 0)
-    shares = lax.axis_size("leaf") * lax.axis_size("col")
-    share_rows = rows_dev // shares
-    share_at = group_at * lax.axis_size("col") + col_at
-    root_share = lax.dynamic_slice_in_dim(root_block, share_at * share_rows, share_rows, 0)
-    root_full = lax.all_gather(root_share, ("row", "leaf", "col"), axis=0, tiled=True)
-
-    panel_quarter = lax.all_gather(second_panels[0], "row", axis=0, tiled=True)
-    panel_half = both_columns(panel_quarter, col_at, 1)
+    count = lax.axis_size("row")
+    mine = jnp.zeros((count, rows_dev, half_cols), jnp.bfloat16)
+    other = mine
+    for apart in range(count):
+        came = second_panels[0]
+        if apart > 0:
+            came = lax.ppermute(came, "row", row_route(apart))
+        mine = lax.dynamic_update_index_in_dim(mine, came, row_at ^ apart, 0)
+        other = lax.dynamic_update_index_in_dim(other, swap_columns(came), row_at ^ apart, 0)
+    panel_half = beside(mine, other, col_at, 2).reshape(tile_width, 2 * half_cols)
     panel_one = beside(panel_half, partner(panel_half, "leaf", 0), half_at, 1)
     inverse_half = both_columns(second_inverse[0], col_at, 0)
     inverse_one = beside(inverse_half, partner(inverse_half, "leaf", 0), half_at, 0)
@@ -294,10 +316,13 @@
     keep_one = all_index < width_one
     keep_rows_one = row_index < width_one
     off_one = jnp.where(keep_one[None, :], -product(root_block, panel_one), 0).astype(jnp.bfloat16)
-    panel_turn = lax.dynamic_slice_in_dim(panel_one, row_first, rows_dev, 1)
-    turn_one = jnp.where(keep_rows_one[None, :], -product(root_full, panel_turn), 0).astype(
-        jnp.bfloat16
-    )
+    share_rows = rows_dev // 4
+    share_at = 2 * half_at + col_at
+    share = lax.dynamic_slice_in_dim(off_one, share_at * share_rows, share_rows, 0)
+    turn_share = row_exchange(share, row_at)
+    turn_share = both_columns(turn_share, col_at, 1)
+    turn_one = beside(turn_share, partner(turn_share, "leaf", 0), half_at, 1)
+    turn_one = turn_one.reshape(tile_width, rows_dev)
     mask_one = keep_one[:, None] & keep_rows_one[None, :]
     diag_one = jnp.where(
         mask_one, inverse_one.astype(jnp.float32) - inner(panel_one, turn_one), 0
@@ -305,72 +330,98 @@
     quarter_first = half_at * (tile_width // 2) + col_at * half_cols
     second_off = lax.dynamic_slice_in_dim(off_one, quarter_first, half_cols, 1)[None]
     second_diag = lax.dynamic_slice_in_dim(diag_one, quarter_first, half_cols, 0)[None]
-    upper_two = jnp.concatenate([root_block, off_one], 1)
-    lower_two = jnp.concatenate([turn_one, diag_one], 0).T
-    chain_two = jnp.concatenate([upper_two, lower_two], 0)
 
     panel_two = lax.all_gather(third_panels[0], "row", axis=1, tiled=True)
-    panel_two = panel_two.reshape(2 * tile_width, own_cols)
+    panel_root, panel_second = panel_two[0], panel_two[1]
     width_two = node_width(widths, 3 + group_at)
     keep_two = own_index < width_two
     keep_rows_two = row_index < width_two
-    off_two = jnp.where(keep_two[None, :], -product(chain_two, panel_two), 0).astype(jnp.bfloat16)
-    off_two = off_two.reshape(2, rows_dev, own_cols)
-    full_two = both_columns(off_two, col_at, 2)
-    turn_share = lax.dynamic_index_in_dim(full_two, col_at, 0, keepdims=False)
-    turn_share = lax.all_to_all(turn_share, "row", split_axis=1, concat_axis=0, tiled=True)
-    turn_two = both_columns(turn_share, col_at, 0)
     mask_two = keep_two[:, None] & keep_rows_two[None, :]
+    product_root = product(root_block, panel_root) + product(off_one, panel_second)
+    product_second = inner(turn_one, panel_root) + inner(diag_one, panel_second)
+    off_two = jnp.stack(
+        [
+            jnp.where(keep_two[None, :], -part, 0).astype(jnp.bfloat16)
+            for part in (product_root, product_second)
+        ]
+    )
+    kept = lax.dynamic_index_in_dim(off_two, col_at, 0, keepdims=False)
+    given = lax.dynamic_index_in_dim(off_two, 1 - col_at, 0, keepdims=False)
+    share_two = beside(kept, swap_columns(given), col_at, 1)
+    turn_mine = row_exchange(share_two, row_at).reshape(tile_width, rows_dev)
+    turn_two = both_columns(turn_mine, col_at, 0)
+    other_two = beside(given, swap_columns(kept), col_at, 1)
+    full_root = jnp.where(col_at == 0, share_two, other_two)
+    full_second = jnp.where(col_at == 0, other_two, share_two)
     diag_two = jnp.where(
-        mask_two, third_inverse[0].astype(jnp.float32) - inner(panel_two, turn_two), 0
+        mask_two,
+        third_inverse[0].astype(jnp.float32)
+        - inner(panel_two.reshape(2 * tile_width, own_cols), turn_two),
+        0,
     ).astype(jnp.bfloat16)
     diag_full = both_columns(diag_two, col_at, 0)
-    chain_three = jnp.concatenate(
-        [
-            jnp.concatenate([chain_two, full_two.reshape(2 * rows_dev, tile_width)], 1),
-            jnp.concatenate([turn_two, diag_full], 0).T,
-        ],
-        0,
-    )
 
     bottom_dev = bottom_panels.shape[0]
     list_len = bottom_lists.shape[1]
     block_rows = 2 * tile_width // list_len
+    upper_len = list_len - tile_width // block_rows
+    upper_rows = upper_len * block_rows
     dev_blocks = rows_dev // block_rows
-    chain_blocks = (
-        jnp.arange(3)[:, None] * (tile_width // block_rows)
+    upper_blocks = (
+        jnp.arange(2)[:, None] * (tile_width // block_rows)
         + row_at * dev_blocks
         + jnp.arange(dev_blocks)[None, :]
     ).reshape(-1)
-    offs = []
+    from_root = jnp.concatenate([root_block, off_one], 1)
+    from_second = jnp.concatenate([turn_one, diag_one], 0)
+    uppers = []
+    lowers = []
+    panels = []
+    slots = []
+    parent_slots = upper_len + row_at * dev_blocks + jnp.arange(dev_blocks)
+    for at in range(bottom_dev):
+        listed = bottom_lists[at, :upper_len]
+        matches = listed[:, None] == upper_blocks[None, :]
+        member_rows = jnp.repeat(jnp.any(matches, axis=0), block_rows)
+        upper_slots = jnp.sum(jnp.where(matches, jnp.arange(upper_len)[:, None], 0), axis=0)
+        slots.append(jnp.concatenate([upper_slots, parent_slots]).astype(jnp.int32))
+        width_three = node_width(widths, NODES - BOTTOM + bottom_dev * group_at + at)
+        keep_three = own_index < width_three
+        keep_upper = member_rows[:, None] & keep_three[None, :]
+        panel = lax.all_gather(bottom_panels[at], "row", axis=0, tiled=True)
+        top, low = panel[:upper_rows], panel[upper_rows:]
+        listed_root = pick_columns(from_root, listed, block_rows)
+        listed_second = pick_rows(from_second, listed, block_rows)
+        listed_parent = pick_rows(turn_two, listed, block_rows)
+        product_root = product(listed_root, top) + product(full_root, low)
+        product_second = inner(listed_second, top) + product(full_second, low)
+        upper = jnp.concatenate([product_root, product_second], 0)
+        lower = inner(listed_parent, top) + inner(diag_full, low)
+        uppers.append(jnp.where(keep_upper, -upper, 0).astype(jnp.bfloat16))
+        lowers.append(jnp.where(keep_three[None, :], -lower, 0).astype(jnp.bfloat16))
+        panels.append(panel)
+    fulls = []
+    for at in range(bottom_dev):
+        mine = jnp.concatenate([uppers[at], lowers[at]], 0)
+        other = jnp.concatenate([swap_columns(uppers[at]), swap_columns(lowers[at])], 0)
+        fulls.append(beside(mine, other, col_at, 1))
     diags = []
     for at in range(bottom_dev):
-        listed = bottom_lists[at]
-        matches = listed[:, None] == chain_blocks[None, :]
-        member = jnp.any(matches, axis=0)
-        slots = jnp.sum(jnp.where(matches, jnp.arange(list_len)[:, None], 0), axis=0)
-        member_rows = jnp.repeat(member, block_rows)
         width_three = node_width(widths, NODES - BOTTOM + bottom_dev * group_at + at)
-        keep_three = own_index < width_three
-        keep_rows_three = row_index < width_three
-        panel_three = lax.all_gather(bottom_panels[at], "row", axis=0, tiled=True)
-        chain_listed = pick_columns(chain_three, listed, block_rows)
-        off_three = jnp.where(
-            member_rows[:, None] & keep_three[None, :], -product(chain_listed, panel_three), 0
-        ).astype(jnp.bfloat16)
-        full_three = both_columns(off_three, col_at, 1)
-        kept_rows = pick_rows(panel_three, slots, block_rows)
-        term_three = inner(kept_rows, full_three).astype(jnp.bfloat16)
-        summed_three = lax.psum_scatter(term_three, "row", scatter_dimension=1, tiled=True)
-        mask_three = keep_three[:, None] & keep_rows_three[None, :]
+        mask_three = (own_index < width_three)[:, None] & (row_index < width_three)[None, :]
+        term = inner(fulls[at], pick_rows(panels[at], slots[at], block_rows))
+        summed = lax.psum_scatter(
+            term.astype(jnp.bfloat16), "row", scatter_dimension=0, tiled=True
+        ).astype(jnp.float32).T
         diags.append(
-            jnp.where(
-                mask_three,
-                bottom_inverse[at].astype(jnp.float32) - summed_three.astype(jnp.float32),
-                0,
-            ).astype(jnp.bfloat16)
+            jnp.where(mask_three, bottom_inverse[at].astype(jnp.float32) - summed, 0).astype(
+                jnp.bfloat16
+            )
         )
-        offs.append(off_three.reshape(3, rows_dev, own_cols))
+    offs = [
+        jnp.concatenate([upper, lower], 0).reshape(3, rows_dev, own_cols)
+        for upper, lower in zip(uppers, lowers)
+    ]
     return (
         second_off,
         second_diag,
@@ -401,5 +452,11 @@
         P("leaf", None, "row", "col"),
         P("leaf", "col", "row"),
     )
-    body = local_paired if mesh.shape["col"] == 2 else local_general
-    return jax.shard_map(body, mesh=mesh, in_specs=in_specs, out_specs=out_specs, check_vma=False)
+    if mesh.shape["col"] != 2:
+        return jax.shard_map(
+            local_general, mesh=mesh, in_specs=in_specs, out_specs=out_specs, check_vma=False
+        )
+
+    return jax.shard_map(
+        local_paired, mesh=mesh, in_specs=in_specs, out_specs=out_specs, check_vma=False
+    )

time: 939 us -> 755 us (0.80)
  waiting for transfers between devices: 500 us -> 342 us
  blocking collectives: 107 us -> 0 us
  starting transfers between devices: 10.8 us -> 76.3 us
  other arithmetic: 83.6 us -> 48.3 us
  matrix products: 120 us -> 138 us
  Pallas kernels: 61 us -> 78.9 us
  local copies, waits for them, and re-layouts: 36.4 us -> 48.5 us
    all_gather x1, waiting for transfers between devices: 120 us -> 0.02 us  [local_paired(): panel_two = lax.all_gather(third_panels[0], 'row', axis=1, tiled=True)]
    all_to_all x1 -> x0, blocking collectives: 107 us -> none  [local_paired(): lax.all_to_all(turn_share, 'row', split_axis=1, concat_axis=0, tiled=True)]
    ppermute x7 -> x23, starting transfers between devices: 10.3 us -> 75.4 us  [the longest x6 50.6 us: row_exchange(): came = lax.ppermute(sent, 'row', row_route(apart))]
    ppermute x7 -> x23, waiting for transfers between devices: 280 us -> 233 us  [the longest x14 112 us: swap_columns(): return lax.ppermute(block, 'col', [(0, 1), (1, 0)])]
    dot_general x4 -> x12, matrix products: 45.5 us -> 90.8 us  [inner(): lax.dot_general(left, right, (((0,), (0,)), ((), ())), preferred_element_...]
    pallas_call x2 -> x6, Pallas kernels: 17.2 us -> 58.4 us  [pick_rows(): pl.pallas_call(copy_block, out_shape=jax.ShapeDtypeStruct((count * height...]
    dot_general x5 -> x9, matrix products: 74.7 us -> 46.9 us  [product(): return jnp.dot(left, right, preferred_element_type=jnp.float32)]
    pallas_call x2, Pallas kernels: 43.8 us -> 20.4 us  [pick_columns(): pl.pallas_call(copy_block, out_shape=jax.ShapeDtypeStruct((rows, count *...]
  transfers between devices with their start and end apart: 16 -> 31, of which waited for: 10 -> 22; matrix products, arithmetic and copies ran while one was open for 25% -> 30% of each run, Pallas kernels for 7% -> 11%
where the time goes in v2:
time: 755 us; the launch traced here: 746 us
  waiting for transfers between devices  342 us (45%)
  matrix products  138 us (18%)
  Pallas kernels  78.9 us (10%)
  starting transfers between devices  76.3 us (10%)
  local copies, waits for them, and re-layouts  48.5 us (6%)
  other arithmetic  48.3 us (6%)
  between operations  14.8 us (2%)
    ppermute x14, waiting for transfers between devices, swap_columns(): return lax.ppermute(block, 'col', [(0, 1), (1, 0)])  112 us
    dot_general x12, matrix products, inner(): lax.dot_general(left, right, (((0,), (0,)), ((), ())), preferred_element_...  90.8 us
    ppermute x6, waiting for transfers between devices, row_exchange(): came = lax.ppermute(sent, 'row', row_route(apart))  65.5 us
    pallas_call x6, Pallas kernels, pick_rows(): pl.pallas_call(copy_block, out_shape=jax.ShapeDtypeStruct((count * height...  58.4 us
    all_gather x2, waiting for transfers between devices, local_paired(): panel = lax.all_gather(bottom_panels[at], 'row', axis=0, tiled=True)  57.4 us
    ppermute x3, waiting for transfers between devices, local_paired(): came = lax.ppermute(came, 'row', row_route(apart))  55.6 us
    ppermute x6, starting transfers between devices, row_exchange(): came = lax.ppermute(sent, 'row', row_route(apart))  50.6 us
    reduce_scatter x2, waiting for transfers between devices, local_paired(): lax.psum_scatter(term.astype(jnp.bfloat16), 'row', scatter_dimension=0, t...  48.3 us
  transfers between devices with their start and end apart: 31, of which 22 were waited for; matrix products, arithmetic and copies ran while one was open for 30% of the time, Pallas kernels for 11%

profile of v2, /device:TPU:0, one launch (start us, length us, event | category | flops | bytes accessed | tf_op | source)
XLA Modules:
  0.0 746.5 jit_solution(13922907494594903533)
XLA Ops:
  8.0 4.7 fusion.83
  12.7 3.1 collective-permute-start
  15.9 2.6 collective-permute-start.1
  20.4 32.5 %collective-permute-done = bf16[512,512]{1,0:T(8,128)(2,1)S(1)} collective-permute-done((bf16[512,512]{1,0:T(8,128)(2,1)S(1)}, bf16[512,512]{1,0:T(8,128)(2,1)S(1)}, u32[]{:S(2)}, u32[]{:S(2)}) %collective-permute-start) | collective-permute-done | bytes 524320 | tf_op jit(solution)/shard_map/ppermute | solution.py:307
  55.1 7.0 collective-permute-done.1
  63.7 16.0 %collective-permute-done.2 = bf16[512,512]{1,0:T(8,128)(2,1)S(1)} collective-permute-done((bf16[512,512]{1,0:T(8,128)(2,1)S(1)}, bf16[512,512]{1,0:T(8,128)(2,1)S(1)}, u32[]{:S(2)}, u32[]{:S(2)}) %collective-permute-start.2) | collective-permute-done | bytes 524320 | tf_op jit(solution)/shard_map/ppermute | solution.py:307
  81.8 8.5 %collective-permute-done.6 = bf16[512,512]{1,0:T(8,128)(2,1)S(1)} collective-permute-done((bf16[512,512]{1,0:T(8,128)(2,1)S(1)}, bf16[512,512]{1,0:T(8,128)(2,1)S(1)}, u32[]{:S(2)}, u32[]{:S(2)}) %collective-permute-start.6) | collective-permute-done | bytes 524320 | tf_op jit(solution)/shard_map/ppermute | solution.py:239
  90.3 2.7 maximum_select_fusion.5
  98.1 2.4 collective-permute-done.7
  100.5 10.9 %select_convert_fusion.1 = bf16[512,2048]{1,0:T(8,128)(2,1)S(1)} fusion(bf16[512,2048]{1,0:T(8,128)(2,1)S(1)} %and_select_fusion, pred[2048]{0:T(1024)(128)(4,1)S(1)} %iota_compare_fusion.1, bf16[2048,1024]{1,0:T(8,128)(2,1)} %collective-permute-done.7, bf16[2048,1024]{1,0:T(8,128)(2,1)} %maximum_select_fusion.5, pred[]{:T(512)S(6)} %eq.41), kind=kOutput, calls=%fused_computation.43 | convolution fusion | flops 4335861760 | bytes 12584961 | tf_op jit(solution)/shard_map/dot_general | solution.py:264
  113.0 34.2 %collective-permute-start.10 = (bf16[128,512]{1,0:T(8,128)(2,1)S(1)}, bf16[128,512]{1,0:T(8,128)(2,1)S(1)}, u32[]{:S(2)}, u32[]{:S(2)}) collective-permute-start(bf16[128,512]{1,0:T(8,128)(2,1)S(1)} %get-tuple-element.38), channel_id=1, source_target_pairs={{0,2},{2,0},{4,6},{6,4},{1,3},{3,1},{5,7},{7,5},{8,10},{10,8},{12,... | collective-permute-start | bytes 393224 | tf_op jit(solution)/shard_map/ppermute | solution.py:258
  151.7 10.4 %collective-permute-done.10 = bf16[128,512]{1,0:T(8,128)(2,1)S(1)} collective-permute-done((bf16[128,512]{1,0:T(8,128)(2,1)S(1)}, bf16[128,512]{1,0:T(8,128)(2,1)S(1)}, u32[]{:S(2)}, u32[]{:S(2)}) %collective-permute-start.10) | collective-permute-done | bytes 131104 | tf_op jit(solution)/shard_map/ppermute | solution.py:258
  162.2 6.3 collective-permute-done.11
  170.9 12.8 %collective-permute-done.13 = bf16[4,128,512]{2,1,0:T(8,128)(2,1)S(1)} collective-permute-done((bf16[4,128,512]{2,1,0:T(8,128)(2,1)S(1)}, bf16[4,128,512]{2,1,0:T(8,128)(2,1)S(1)}, u32[]{:S(2)}, u32[]{:S(2)}) %collective-permute-start.13) | collective-permute-done | bytes 524320 | tf_op jit(solution)/shard_map/ppermute | solution.py:239
  184.2 9.1 %collective-permute-done.8 = bf16[512,512]{1,0:T(8,128)(2,1)S(1)} collective-permute-done((bf16[512,512]{1,0:T(8,128)(2,1)}, bf16[512,512]{1,0:T(8,128)(2,1)S(1)}, u32[]{:S(2)}, u32[]{:S(2)}) %collective-permute-start.8) | collective-permute-done | bytes 524320 | tf_op jit(solution)/shard_map/ppermute | solution.py:239
  193.3 2.6 maximum_select_fusion.18
  197.8 3.5 maximum_select_fusion.12
  201.3 17.1 %select_convert_fusion = bf16[2048,512]{1,0:T(8,128)(2,1)} fusion(bf16[1024,512]{1,0:T(8,128)(2,1)} %collective-permute-done.9, bf16[1024,512]{1,0:T(8,128)(2,1)} %maximum_select_fusion.18, pred[]{:T(512)S(6)} %eq.41, pred[512]{0:T(512)(128)(4,1)S(1)} %fusion.70, pred[2048]{0:T(1024)(128)(4,1)S(1)} %iota_compare_fusion.1, bf16[2048,512]{1,0:T(8,128)(2,1)} %bitcast.155, ...), kind=kOutput, calls=%fused_computation.42 | convolution fusion | flops 4347396096 | bytes 14682625 | tf_op jit(solution)/shard_map/dot_general | solution.py:268
  218.5 5.2 fusion.29
  225.3 2.4 fusion.30
  239.0 20.0 %collective-permute-done.15 = bf16[512,1024]{1,0:T(8,128)(2,1)S(1)} collective-permute-done((bf16[512,1024]{1,0:T(8,128)(2,1)S(1)}, bf16[512,1024]{1,0:T(8,128)(2,1)S(1)}, u32[]{:S(2)}, u32[]{:S(2)}) %collective-permute-start.15) | collective-permute-done | bytes 1048608 | tf_op jit(solution)/shard_map/ppermute | solution.py:239
  260.1 2.5 maximum_select_fusion.13
  263.7 9.5 %collective-permute-start.16 = (bf16[512,512]{1,0:T(8,128)(2,1)}, bf16[512,512]{1,0:T(8,128)(2,1)}, u32[]{:S(2)}, u32[]{:S(2)}) collective-permute-start(bf16[512,512]{1,0:T(8,128)(2,1)} %get-tuple-element.33), channel_id=1, source_target_pairs={{0,2},{2,0},{4,6},{6,4},{1,3},{3,1},{5,7},{7,5},{8,10},{10,8},{12,... | collective-permute-start | bytes 1572872 | tf_op jit(solution)/shard_map/ppermute | solution.py:258
  275.2 2.6 pad_maximum_fusion.1.blocks_in
  277.8 10.2 %pick_columns.3 = bf16[512,2048]{1,0:T(8,128)(2,1)} custom-call(s32[16]{0:T(128)} %copy-done.33, bf16[512,4096]{1,0:T(8,128)(2,1)} %pad_maximum_fusion.1.blocks_in), custom_call_target="tpu_custom_call" | custom-call | bytes 4194304 | tf_op jit(solution)/shard_map/pick_columns/pallas_call | solution.py:195
  293.3 26.4 %collective-permute-done.16 = bf16[512,512]{1,0:T(8,128)(2,1)} collective-permute-done((bf16[512,512]{1,0:T(8,128)(2,1)}, bf16[512,512]{1,0:T(8,128)(2,1)}, u32[]{:S(2)}, u32[]{:S(2)}) %collective-permute-start.16) | collective-permute-done | bytes 524320 | tf_op jit(solution)/shard_map/ppermute | solution.py:258
  325.0 20.5 %collective-permute-done.18 = bf16[512,512]{1,0:T(8,128)(2,1)S(1)} collective-permute-done((bf16[512,512]{1,0:T(8,128)(2,1)}, bf16[512,512]{1,0:T(8,128)(2,1)S(1)}, u32[]{:S(2)}, u32[]{:S(2)}) %collective-permute-start.18) | collective-permute-done | bytes 524320 | tf_op jit(solution)/shard_map/ppermute | solution.py:258
  350.0 10.5 %pick_rows.8 = bf16[2048,512]{1,0:T(8,128)(2,1)} custom-call(s32[16]{0:T(128)} %copy-done.33, bf16[4096,512]{1,0:T(8,128)(2,1)} %pad_maximum_fusion.2.blocks_in), custom_call_target="tpu_custom_call" | custom-call | bytes 4194304 | tf_op jit(solution)/shard_map/pick_rows/pallas_call | solution.py:214
  360.5 46.0 %all-gather.11.cloned.1.call-done = bf16[1,4096,1024]{2,1,0:T(8,128)(2,1)} async-done(((bf16[1,1024,1024]{2,1,0:T(8,128)(2,1)}), bf16[1,4096,1024]{2,1,0:T(8,128)(2,1)}) %all-gather.11.cloned.1.call-update) | async-done | bytes 8388624 | tf_op jit(solution)/shard_map/all_gather | solution.py:391
  406.5 4.7 fusion.40
  411.6 5.5 fusion.51
  417.1 4.5 maximum_select_fusion.6.blocks_in
  421.7 5.7 fusion.50
  428.9 4.1 fusion.42
  436.7 10.2 %pick_rows.9 = bf16[2048,512]{1,0:T(8,128)(2,1)} custom-call(s32[16]{0:T(128)} %copy-done.33, bf16[4096,512]{1,0:T(8,128)(2,1)} %copy-done), custom_call_target="tpu_custom_call" | custom-call | bytes 4194304 | tf_op jit(solution)/shard_map/pick_rows/pallas_call | solution.py:214
  446.9 6.9 collective-permute-done.21
  453.8 5.9 fusion.41
  459.6 5.5 select_convert_fusion.2
  468.2 10.2 %pick_columns.2 = bf16[512,2048]{1,0:T(8,128)(2,1)} custom-call(s32[16]{0:T(128)} %copy-done.32, bf16[512,4096]{1,0:T(8,128)(2,1)} %pad_maximum_fusion.1.blocks_in), custom_call_target="tpu_custom_call" | custom-call | bytes 4194304 | tf_op jit(solution)/shard_map/pick_columns/pallas_call | solution.py:195
  478.4 10.2 %pick_rows.6 = bf16[2048,512]{1,0:T(8,128)(2,1)} custom-call(s32[16]{0:T(128)} %copy-done.32, bf16[4096,512]{1,0:T(8,128)(2,1)} %pad_maximum_fusion.2.blocks_in), custom_call_target="tpu_custom_call" | custom-call | bytes 4194304 | tf_op jit(solution)/shard_map/pick_rows/pallas_call | solution.py:214
  488.5 8.6 %pick_rows.11 = bf16[1536,1024]{1,0:T(8,128)(2,1)} custom-call(s32[12]{0:T(128)} %get-tuple-element.42.picks, bf16[4096,1024]{1,0:T(8,128)(2,1)} %bitcast.153), custom_call_target="tpu_custom_call" | custom-call | bytes 6291456 | tf_op jit(solution)/shard_map/pick_rows/pallas_call | solution.py:214
  498.7 3.0 constant_dynamic-update-slice_fusion.3
  501.8 18.5 %collective-permute-done.25 = bf16[512,1024]{1,0:T(8,128)(2,1)} collective-permute-done((bf16[512,1024]{1,0:T(8,128)(2,1)}, bf16[512,1024]{1,0:T(8,128)(2,1)}, u32[]{:S(2)}, u32[]{:S(2)}) %collective-permute-start.25) | collective-permute-done | bytes 1048608 | tf_op jit(solution)/shard_map/ppermute | solution.py:239
  522.5 21.6 %fusion.26 = bf16[2048,1024]{1,0:T(8,128)(2,1)} fusion(bf16[1536,1024]{1,0:T(8,128)(2,1)S(1)} %copy-done.18, bf16[1536,1024]{1,0:T(8,128)(2,1)} %constant_dynamic-update-slice_fusion.2, bf16[512,1024]{1,0:T(8,128)(2,1)} %select_convert_fusion.2, bf16[1024,1024]{1,0:T(8,128)(2,1)S(1)} %fusion.25, pred[]{:T(512)S(6)} %eq.42), kind=kOutput, calls=%fused_computation.45 | convolution fusion | flops 6485442560 | bytes 13631489 | tf_op jit(solution)/shard_map/dot_general | solution.py:268
  544.4 11.4 %all-gather.9.cloned.1.call-done = bf16[1,4096,1024]{2,1,0:T(8,128)(2,1)} async-done(((bf16[1,1024,1024]{2,1,0:T(8,128)(2,1)}), bf16[1,4096,1024]{2,1,0:T(8,128)(2,1)}) %all-gather.9.cloned.1.call-update) | async-done | bytes 8388624 | tf_op jit(solution)/shard_map/all_gather | solution.py:391
  555.8 5.3 fusion.34
  561.6 4.7 fusion.36
  566.3 2.4 fusion.87
  568.7 4.1 fusion.52
  576.4 10.4 %pick_rows.7 = bf16[2048,512]{1,0:T(8,128)(2,1)} custom-call(s32[16]{0:T(128)} %copy-done.32, bf16[4096,512]{1,0:T(8,128)(2,1)} %copy-done), custom_call_target="tpu_custom_call" | custom-call | bytes 4194304 | tf_op jit(solution)/shard_map/pick_rows/pallas_call | solution.py:214
  586.7 6.0 fusion.35
  592.7 5.5 select_convert_fusion.3
  598.7 8.7 %pick_rows.10 = bf16[1536,1024]{1,0:T(8,128)(2,1)} custom-call(s32[12]{0:T(128)} %get-tuple-element.41.picks, bf16[4096,1024]{1,0:T(8,128)(2,1)} %bitcast.154), custom_call_target="tpu_custom_call" | custom-call | bytes 6291456 | tf_op jit(solution)/shard_map/pick_rows/pallas_call | solution.py:214
  607.3 16.3 %collective-permute-done.22 = bf16[1024,1024]{1,0:T(8,128)(2,1)} collective-permute-done((bf16[1024,1024]{1,0:T(8,128)(2,1)}, bf16[1024,1024]{1,0:T(8,128)(2,1)}, u32[]{:S(2)}, u32[]{:S(2)}) %collective-permute-start.22) | collective-permute-done | bytes 2097184 | tf_op jit(solution)/shard_map/ppermute | solution.py:239
  623.6 3.1 constant_dynamic-update-slice_fusion.1
  626.7 18.4 %collective-permute-done.23 = bf16[512,1024]{1,0:T(8,128)(2,1)S(1)} collective-permute-done((bf16[512,1024]{1,0:T(8,128)(2,1)}, bf16[512,1024]{1,0:T(8,128)(2,1)S(1)}, u32[]{:S(2)}, u32[]{:S(2)}) %collective-permute-start.23) | collective-permute-done | bytes 1048608 | tf_op jit(solution)/shard_map/ppermute | solution.py:239
  646.2 14.0 %fusion.27 = bf16[2048,1024]{1,0:T(8,128)(2,1)} fusion(bf16[1536,1024]{1,0:T(8,128)(2,1)S(1)} %copy-done.17, bf16[1536,1024]{1,0:T(8,128)(2,1)} %constant_dynamic-update-slice_fusion, bf16[512,1024]{1,0:T(8,128)(2,1)} %select_convert_fusion.3, bf16[1024,1024]{1,0:T(8,128)(2,1)} %fusion.23, pred[]{:T(512)S(6)} %eq.42), kind=kOutput, calls=%fused_computation.46 | convolution fusion | flops 6485442560 | bytes 13631489 | tf_op jit(solution)/shard_map/dot_general | solution.py:268
  660.2 3.0 fusion.84
  663.2 2.4 copy.26
  672.9 2.8 fusion.44
  675.7 2.5 copy.23
  681.9 3.2 pad_maximum_fusion
  687.0 48.3 %reduce-scatter.3.cloned.1.call-done = bf16[512,1024]{1,0:T(8,128)(2,1)} async-done(((bf16[2048,1024]{1,0:T(8,128)(2,1)}), bf16[512,1024]{1,0:T(8,128)(2,1)}) %reduce-scatter.3.cloned.1.call-update) | async-done | bytes 1048592 | tf_op jit(solution)/shard_map/reduce_scatter | solution.py:413
  737.1 2.6 copy.24
  (187 shorter events, 89.4 us)
Async XLA Ops:
  7.2 211.3 %all-gather.7.cloned.1.call-start = ((), (), s32[]{:S(2)}) async-start(), calls=%async_computation.4 | async-start | bytes 10485760 | tf_op jit(solution)/shard_map/all_gather | solution.py:334
  7.9 4.8 copy-start.31
  7.9 398.5 %all-gather.11.cloned.1.call-start = ((), (), s32[]{:S(2)}) async-start(), calls=%async_computation.6 | async-start | bytes 10485760 | tf_op jit(solution)/shard_map/all_gather | solution.py:391
  12.7 543.1 %all-gather.9.cloned.1.call-start = ((), (), s32[]{:S(2)}) async-start(), calls=%async_computation.5 | async-start | bytes 10485760 | tf_op jit(solution)/shard_map/all_gather | solution.py:391
  12.7 40.2 %collective-permute-start = (bf16[512,512]{1,0:T(8,128)(2,1)S(1)}, bf16[512,512]{1,0:T(8,128)(2,1)S(1)}, u32[]{:S(2)}, u32[]{:S(2)}) collective-permute-start(bf16[512,512]{1,0:T(8,128)(2,1)S(1)} %bitcast.160), channel_id=1, source_target_pairs={{0,2},{2,0},{4,6},{6,4},{1,3},{3,1},{5,7},{7,5},{8,10},{10,8},{12,... | collective-permute-start | bytes 1572872 | tf_op jit(solution)/shard_map/ppermute | solution.py:307
  15.9 46.3 %collective-permute-start.1 = (bf16[512,512]{1,0:T(8,128)(2,1)S(1)}, bf16[512,512]{1,0:T(8,128)(2,1)S(1)}, u32[]{:S(2)}, u32[]{:S(2)}) collective-permute-start(bf16[512,512]{1,0:T(8,128)(2,1)S(1)} %bitcast.161), channel_id=1, source_target_pairs={{0,4},{2,6},{4,0},{6,2},{1,5},{3,7},{5,1},{7,3},{8,12},{10,14},{12... | collective-permute-start | bytes 1572872 | tf_op jit(solution)/shard_map/ppermute | solution.py:307
  18.4 61.3 %collective-permute-start.2 = (bf16[512,512]{1,0:T(8,128)(2,1)S(1)}, bf16[512,512]{1,0:T(8,128)(2,1)S(1)}, u32[]{:S(2)}, u32[]{:S(2)}) collective-permute-start(bf16[512,512]{1,0:T(8,128)(2,1)S(1)} %bitcast.162), channel_id=1, source_target_pairs={{0,6},{2,4},{4,2},{6,0},{1,7},{3,5},{5,3},{7,1},{8,14},{10,12},{12... | collective-permute-start | bytes 1572872 | tf_op jit(solution)/shard_map/ppermute | solution.py:307
  18.5 62.8 %collective-permute-start.3 = (bf16[512,512]{1,0:T(8,128)(2,1)S(1)}, bf16[512,512]{1,0:T(8,128)(2,1)S(1)}, u32[]{:S(2)}, u32[]{:S(2)}) collective-permute-start(bf16[512,512]{1,0:T(8,128)(2,1)S(1)} %bitcast.163), channel_id=1, source_target_pairs={{0,1},{1,0},{2,3},{3,2},{4,5},{5,4},{6,7},{7,6},{8,9},{9,8},{10,11... | collective-permute-start | bytes 1572872 | tf_op jit(solution)/shard_map/ppermute | solution.py:239
  52.9 28.7 %collective-permute-start.4 = (bf16[512,512]{1,0:T(8,128)(2,1)S(1)}, bf16[512,512]{1,0:T(8,128)(2,1)S(1)}, u32[]{:S(2)}, u32[]{:S(2)}) collective-permute-start(bf16[512,512]{1,0:T(8,128)(2,1)S(1)} %collective-permute-done), channel_id=1, source_target_pairs={{0,1},{1,0},{2,3},{3,2},{4,5},{5,4},{6,7},{7,6},{8,9},{9,8},{10,11... | collective-permute-start | bytes 1572872 | tf_op jit(solution)/shard_map/ppermute | solution.py:239
  62.1 19.6 %collective-permute-start.5 = (bf16[512,512]{1,0:T(8,128)(2,1)S(1)}, bf16[512,512]{1,0:T(8,128)(2,1)S(1)}, u32[]{:S(2)}, u32[]{:S(2)}) collective-permute-start(bf16[512,512]{1,0:T(8,128)(2,1)S(1)} %collective-permute-done.1), channel_id=1, source_target_pairs={{0,1},{1,0},{2,3},{3,2},{4,5},{5,4},{6,7},{7,6},{8,9},{9,8},{10,11... | collective-permute-start | bytes 1572872 | tf_op jit(solution)/shard_map/ppermute | solution.py:239
  79.7 10.5 %collective-permute-start.6 = (bf16[512,512]{1,0:T(8,128)(2,1)S(1)}, bf16[512,512]{1,0:T(8,128)(2,1)S(1)}, u32[]{:S(2)}, u32[]{:S(2)}) collective-permute-start(bf16[512,512]{1,0:T(8,128)(2,1)S(1)} %collective-permute-done.2), channel_id=1, source_target_pairs={{0,1},{1,0},{2,3},{3,2},{4,5},{5,4},{6,7},{7,6},{8,9},{9,8},{10,11... | collective-permute-start | bytes 1572872 | tf_op jit(solution)/shard_map/ppermute | solution.py:239
  93.0 7.5 %collective-permute-start.7 = (bf16[2048,1024]{1,0:T(8,128)(2,1)}, bf16[2048,1024]{1,0:T(8,128)(2,1)}, u32[]{:S(2)}, u32[]{:S(2)}) collective-permute-start(bf16[2048,1024]{1,0:T(8,128)(2,1)} %maximum_select_fusion.5), channel_id=1, source_target_pairs={{0,8},{8,0},{16,24},{24,16},{1,9},{9,1},{17,25},{25,17},{2,10},{10... | collective-permute-start | bytes 12582920 | tf_op jit(solution)/shard_map/ppermute | solution.py:19
  98.1 120.4 %copy-start.3 = (bf16[512,2048]{1,0:T(8,128)(2,1)}, bf16[512,2048]{1,0:T(8,128)(2,1)S(1)}, u32[]{:S(2)}) copy-start(bf16[512,2048]{1,0:T(8,128)(2,1)S(1)} %and_select_fusion) | copy-start | bytes 6291460
  113.0 49.1 %collective-permute-start.10 = (bf16[128,512]{1,0:T(8,128)(2,1)S(1)}, bf16[128,512]{1,0:T(8,128)(2,1)S(1)}, u32[]{:S(2)}, u32[]{:S(2)}) collective-permute-start(bf16[128,512]{1,0:T(8,128)(2,1)S(1)} %get-tuple-element.38), channel_id=1, source_target_pairs={{0,2},{2,0},{4,6},{6,4},{1,3},{3,1},{5,7},{7,5},{8,10},{10,8},{12,... | collective-permute-start | bytes 393224 | tf_op jit(solution)/shard_map/ppermute | solution.py:258
  147.2 21.2 %collective-permute-start.11 = (bf16[128,512]{1,0:T(8,128)(2,1)S(1)}, bf16[128,512]{1,0:T(8,128)(2,1)S(1)}, u32[]{:S(2)}, u32[]{:S(2)}) collective-permute-start(bf16[128,512]{1,0:T(8,128)(2,1)S(1)} %get-tuple-element.37), channel_id=1, source_target_pairs={{0,4},{2,6},{4,0},{6,2},{1,5},{3,7},{5,1},{7,3},{8,12},{10,14},{12... | collective-permute-start | bytes 393224 | tf_op jit(solution)/shard_map/ppermute | solution.py:258
  149.2 19.5 %collective-permute-start.12 = (bf16[128,512]{1,0:T(8,128)(2,1)S(1)}, bf16[128,512]{1,0:T(8,128)(2,1)S(1)}, u32[]{:S(2)}, u32[]{:S(2)}) collective-permute-start(bf16[128,512]{1,0:T(8,128)(2,1)S(1)} %get-tuple-element.36), channel_id=1, source_target_pairs={{0,6},{2,4},{4,2},{6,0},{1,7},{3,5},{5,3},{7,1},{8,14},{10,12},{12... | collective-permute-start | bytes 393224 | tf_op jit(solution)/shard_map/ppermute | solution.py:258
  168.8 14.9 %collective-permute-start.13 = (bf16[4,128,512]{2,1,0:T(8,128)(2,1)S(1)}, bf16[4,128,512]{2,1,0:T(8,128)(2,1)S(1)}, u32[]{:S(2)}, u32[]{:S(2)}) collective-permute-start(bf16[4,128,512]{2,1,0:T(8,128)(2,1)S(1)} %bitcast_dynamic-update-slice_fusion.11), channel_id=1, source_target_pairs={{0,1},{1,0},{2,3},{3,2},{4,5},{5,4},{6,7},{7,6},{8,9},{9,8},{10,11... | collective-permute-start | bytes 1572872 | tf_op jit(solution)/shard_map/ppermute | solution.py:239
  170.3 23.0 %collective-permute-start.8 = (bf16[512,512]{1,0:T(8,128)(2,1)}, bf16[512,512]{1,0:T(8,128)(2,1)S(1)}, u32[]{:S(2)}, u32[]{:S(2)}) collective-permute-start(bf16[512,512]{1,0:T(8,128)(2,1)} %bitcast.11), channel_id=1, source_target_pairs={{0,1},{1,0},{2,3},{3,2},{4,5},{5,4},{6,7},{7,6},{8,9},{9,8},{10,11... | collective-permute-start | bytes 1572872 | tf_op jit(solution)/shard_map/ppermute | solution.py:239
  184.1 13.7 %collective-permute-start.14 = (bf16[4,256,512]{2,1,0:T(8,128)(2,1)S(1)}, bf16[4,256,512]{2,1,0:T(8,128)(2,1)}, u32[]{:S(2)}, u32[]{:S(2)}) collective-permute-start(bf16[4,256,512]{2,1,0:T(8,128)(2,1)S(1)} %maximum_select_fusion.19), channel_id=1, source_target_pairs={{0,8},{8,0},{16,24},{24,16},{1,9},{9,1},{17,25},{25,17},{2,10},{10... | collective-permute-start | bytes 3145736 | tf_op jit(solution)/shard_map/ppermute | solution.py:19
  195.9 5.4 collective-permute-start.9
  195.9 489.3 %reduce-scatter.5.cloned.1.call-start = ((), (), s32[]{:S(2)}) async-start(), calls=%async_computation.3 | async-start | bytes 5242880 | tf_op jit(solution)/shard_map/reduce_scatter | solution.py:413
  218.5 5.3 copy-start.15
  218.5 6.9 copy-start.37
  232.5 6.2 copy-start.35
  233.5 25.6 %copy-start.24 = (bf16[512,1024]{1,0:T(8,128)(2,1)}, bf16[512,1024]{1,0:T(8,128)(2,1)S(1)}, u32[]{:S(2)}) copy-start(bf16[512,1024]{1,0:T(8,128)(2,1)S(1)} %get-tuple-element.35) | copy-start | bytes 3145732
  233.5 25.6 %collective-permute-start.15 = (bf16[512,1024]{1,0:T(8,128)(2,1)S(1)}, bf16[512,1024]{1,0:T(8,128)(2,1)S(1)}, u32[]{:S(2)}, u32[]{:S(2)}) collective-permute-start(bf16[512,1024]{1,0:T(8,128)(2,1)S(1)} %get-tuple-element.35), channel_id=1, source_target_pairs={{0,1},{1,0},{2,3},{3,2},{4,5},{5,4},{6,7},{7,6},{8,9},{9,8},{10,11... | collective-permute-start | bytes 3145736 | tf_op jit(solution)/shard_map/ppermute | solution.py:239
  238.7 25.0 %copy-start.33 = (s32[16]{0:T(128)}, s32[16]{0:T(128)S(1)}, u32[]{:S(2)}) copy-start(s32[16]{0:T(128)S(1)} %get-tuple-element.40.picks) | copy-start | bytes 196
  238.7 228.6 %copy-start.32 = (s32[16]{0:T(128)}, s32[16]{0:T(128)S(1)}, u32[]{:S(2)}) copy-start(s32[16]{0:T(128)S(1)} %get-tuple-element.39.picks) | copy-start | bytes 196
  260.1 15.2 %copy-start.4 = (bf16[512,2048]{1,0:T(8,128)(2,1)S(1)}, bf16[512,2048]{1,0:T(8,128)(2,1)}, u32[]{:S(2)}) copy-start(bf16[512,2048]{1,0:T(8,128)(2,1)} %copy-done.3) | copy-start | bytes 6291460
  260.1 15.2 %copy-start.9 = (bf16[512,2048]{1,0:T(8,128)(2,1)S(1)}, bf16[512,2048]{1,0:T(8,128)(2,1)}, u32[]{:S(2)}) copy-start(bf16[512,2048]{1,0:T(8,128)(2,1)} %copy-done.7) | copy-start | bytes 6291460
  263.7 55.9 %collective-permute-start.16 = (bf16[512,512]{1,0:T(8,128)(2,1)}, bf16[512,512]{1,0:T(8,128)(2,1)}, u32[]{:S(2)}, u32[]{:S(2)}) collective-permute-start(bf16[512,512]{1,0:T(8,128)(2,1)} %get-tuple-element.33), channel_id=1, source_target_pairs={{0,2},{2,0},{4,6},{6,4},{1,3},{3,1},{5,7},{7,5},{8,10},{10,8},{12,... | collective-permute-start | bytes 1572872 | tf_op jit(solution)/shard_map/ppermute | solution.py:258
  273.2 49.9 %collective-permute-start.17 = (bf16[512,512]{1,0:T(8,128)(2,1)}, bf16[512,512]{1,0:T(8,128)(2,1)}, u32[]{:S(2)}, u32[]{:S(2)}) collective-permute-start(bf16[512,512]{1,0:T(8,128)(2,1)} %get-tuple-element.32), channel_id=1, source_target_pairs={{0,4},{2,6},{4,0},{6,2},{1,5},{3,7},{5,1},{7,3},{8,12},{10,14},{12... | collective-permute-start | bytes 1572872 | tf_op jit(solution)/shard_map/ppermute | solution.py:258
  288.0 123.1 %collective-permute-start.20 = (bf16[512,1024]{1,0:T(8,128)(2,1)S(1)}, bf16[512,1024]{1,0:T(8,128)(2,1)}, u32[]{:S(2)}, u32[]{:S(2)}) collective-permute-start(bf16[512,1024]{1,0:T(8,128)(2,1)S(1)} %get-tuple-element.34), channel_id=1, source_target_pairs={{0,1},{1,0},{2,3},{3,2},{4,5},{5,4},{6,7},{7,6},{8,9},{9,8},{10,11... | collective-permute-start | bytes 3145736 | tf_op jit(solution)/shard_map/ppermute | solution.py:239
  289.5 58.3 %copy-start.6 = (bf16[4,512,512]{2,1,0:T(8,128)(2,1)S(1)}, bf16[4,512,512]{2,1,0:T(8,128)(2,1)}, u32[]{:S(2)}) copy-start(bf16[4,512,512]{2,1,0:T(8,128)(2,1)} %maximum_select_fusion.12) | copy-start | bytes 6291460
  289.5 58.3 %copy-start.16 = (bf16[2048,512]{1,0:T(8,128)(2,1)S(1)}, bf16[2048,512]{1,0:T(8,128)(2,1)}, u32[]{:S(2)}) copy-start(bf16[2048,512]{1,0:T(8,128)(2,1)} %select_convert_fusion) | copy-start | bytes 6291460
  289.5 56.0 %collective-permute-start.18 = (bf16[512,512]{1,0:T(8,128)(2,1)}, bf16[512,512]{1,0:T(8,128)(2,1)S(1)}, u32[]{:S(2)}, u32[]{:S(2)}) collective-permute-start(bf16[512,512]{1,0:T(8,128)(2,1)} %get-tuple-element.31), channel_id=1, source_target_pairs={{0,6},{2,4},{4,2},{6,0},{1,7},{3,5},{5,3},{7,1},{8,14},{10,12},{12... | collective-permute-start | bytes 1572872 | tf_op jit(solution)/shard_map/ppermute | solution.py:258
  346.3 70.8 %collective-permute-start.19 = (bf16[2048,512]{1,0:T(8,128)(2,1)}, bf16[2048,512]{1,0:T(8,128)(2,1)}, u32[]{:S(2)}, u32[]{:S(2)}) collective-permute-start(bf16[2048,512]{1,0:T(8,128)(2,1)} %bitcast.30), channel_id=1, source_target_pairs={{0,1},{1,0},{2,3},{3,2},{4,5},{5,4},{6,7},{7,6},{8,9},{9,8},{10,11... | collective-permute-start | bytes 6291464 | tf_op jit(solution)/shard_map/ppermute | solution.py:239
  350.0 56.5 %copy-start.19 = (bf16[512,2048]{1,0:T(8,128)(2,1)S(1)}, bf16[512,2048]{1,0:T(8,128)(2,1)}, u32[]{:S(2)}) copy-start(bf16[512,2048]{1,0:T(8,128)(2,1)} %pick_columns.3) | copy-start | bytes 6291460
  406.4 4.7 copy-start.1
  406.4 4.9 copy-start.25
  406.4 5.2 copy-start.28
  406.5 15.2 %slice-start = ((s8[8388608]{0:T(1024)(128)(4,1)}), s8[4194304]{0:T(1024)(128)(4,1)S(1)}, s32[]{:S(2)}) async-start(s8[8388608]{0:T(1024)(128)(4,1)} %bitcast.164), calls=%async_computation.7 | async-start | bytes 8388608
  411.1 10.5 %slice-start.1 = ((s8[8388608]{0:T(1024)(128)(4,1)}), s8[4194304]{0:T(1024)(128)(4,1)S(1)}, s32[]{:S(2)}) async-start(s8[8388608]{0:T(1024)(128)(4,1)} %bitcast.164), calls=%async_computation.8 | async-start | bytes 8388608
  417.1 4.6 copy-start.30
  421.7 5.8 copy-start
  427.4 5.6 copy-start.21
  427.4 26.3 %collective-permute-start.21 = (bf16[1024,512]{0,1:T(8,128)(2,1)}, bf16[1024,512]{0,1:T(8,128)(2,1)}, u32[]{:S(2)}, u32[]{:S(2)}) collective-permute-start(bf16[1024,512]{0,1:T(8,128)(2,1)} %fusion.50), channel_id=1, source_target_pairs={{0,1},{1,0},{2,3},{3,2},{4,5},{5,4},{6,7},{7,6},{8,9},{9,8},{10,11... | collective-permute-start | bytes 3145736 | tf_op jit(solution)/shard_map/ppermute | solution.py:239
  436.1 62.6 %collective-permute-start.24 = (bf16[1024,1024]{1,0:T(8,128)(2,1)S(1)}, bf16[1024,1024]{1,0:T(8,128)(2,1)}, u32[]{:S(2)}, u32[]{:S(2)}) collective-permute-start(bf16[1024,1024]{1,0:T(8,128)(2,1)S(1)} %fusion.25), channel_id=1, source_target_pairs={{0,1},{1,0},{2,3},{3,2},{4,5},{5,4},{6,7},{7,6},{8,9},{9,8},{10,11... | collective-permute-start | bytes 6291464 | tf_op jit(solution)/shard_map/ppermute | solution.py:239
  446.9 12.8 %copy-start.22 = (bf16[2048,512]{1,0:T(8,128)(2,1)S(1)}, bf16[2048,512]{1,0:T(8,128)(2,1)}, u32[]{:S(2)}) copy-start(bf16[2048,512]{1,0:T(8,128)(2,1)} %pick_rows.9) | copy-start | bytes 6291460
  459.6 7.7 %copy-start.34 = (s32[16]{0:T(128)S(1)}, s32[16]{0:T(128)}, u32[]{:S(2)}) copy-start(s32[16]{0:T(128)} %copy-done.33) | copy-start | bytes 196
  465.2 55.0 %collective-permute-start.25 = (bf16[512,1024]{1,0:T(8,128)(2,1)}, bf16[512,1024]{1,0:T(8,128)(2,1)}, u32[]{:S(2)}, u32[]{:S(2)}) collective-permute-start(bf16[512,1024]{1,0:T(8,128)(2,1)} %select_convert_fusion.2), channel_id=1, source_target_pairs={{0,1},{1,0},{2,3},{3,2},{4,5},{5,4},{6,7},{7,6},{8,9},{9,8},{10,11... | collective-permute-start | bytes 3145736 | tf_op jit(solution)/shard_map/ppermute | solution.py:239
  497.2 25.3 %copy-start.18 = (bf16[1536,1024]{1,0:T(8,128)(2,1)S(1)}, bf16[1536,1024]{1,0:T(8,128)(2,1)}, u32[]{:S(2)}) copy-start(bf16[1536,1024]{1,0:T(8,128)(2,1)} %pick_rows.11) | copy-start | bytes 9437188
  544.1 191.1 %reduce-scatter.3.cloned.1.call-start = ((), (), s32[]{:S(2)}) async-start(), calls=%async_computation.2 | async-start | bytes 5242880 | tf_op jit(solution)/shard_map/reduce_scatter | solution.py:413
  555.8 5.3 copy-start.2
  555.8 5.4 copy-start.26
  555.8 5.7 copy-start.29
  561.6 4.7 copy-start.20
  574.8 48.8 %collective-permute-start.22 = (bf16[1024,1024]{1,0:T(8,128)(2,1)}, bf16[1024,1024]{1,0:T(8,128)(2,1)}, u32[]{:S(2)}, u32[]{:S(2)}) collective-permute-start(bf16[1024,1024]{1,0:T(8,128)(2,1)} %fusion.23), channel_id=1, source_target_pairs={{0,1},{1,0},{2,3},{3,2},{4,5},{5,4},{6,7},{7,6},{8,9},{9,8},{10,11... | collective-permute-start | bytes 6291464 | tf_op jit(solution)/shard_map/ppermute | solution.py:239
  586.7 6.0 copy-start.23
  598.2 46.9 %collective-permute-start.23 = (bf16[512,1024]{1,0:T(8,128)(2,1)}, bf16[512,1024]{1,0:T(8,128)(2,1)S(1)}, u32[]{:S(2)}, u32[]{:S(2)}) collective-permute-start(bf16[512,1024]{1,0:T(8,128)(2,1)} %select_convert_fusion.3), channel_id=1, source_target_pairs={{0,1},{1,0},{2,3},{3,2},{4,5},{5,4},{6,7},{7,6},{8,9},{9,8},{10,11... | collective-permute-start | bytes 3145736 | tf_op jit(solution)/shard_map/ppermute | solution.py:239
  607.3 38.8 %copy-start.17 = (bf16[1536,1024]{1,0:T(8,128)(2,1)S(1)}, bf16[1536,1024]{1,0:T(8,128)(2,1)}, u32[]{:S(2)}) copy-start(bf16[1536,1024]{1,0:T(8,128)(2,1)} %pick_rows.10) | copy-start | bytes 9437188
  663.1 9.7 %copy-start.11 = (bf16[1,512,1024]{2,1,0:T(8,128)(2,1)S(1)}, bf16[1,512,1024]{2,1,0:T(8,128)(2,1)}, u32[]{:S(2)}) copy-start(bf16[1,512,1024]{2,1,0:T(8,128)(2,1)} %copy-done.10) | copy-start | bytes 3145732
  681.9 3.3 copy-start.14
  685.2 50.0 %copy-start.13 = (bf16[1,1024,512]{1,2,0:T(8,128)(2,1)S(1)}, bf16[1,1024,512]{1,2,0:T(8,128)(2,1)}, u32[]{:S(2)}) copy-start(bf16[1,1024,512]{1,2,0:T(8,128)(2,1)} %copy.25) | copy-start | bytes 3145732
  (7 other events, 13.1 us)
Sparse Core Ops, SparseCore 0:
  9.5 200.8 all-gather.6
  212.0 194.3 all-gather.10
  408.0 147.7 all-gather.8
  558.0 74.9 reduce-scatter.4
  660.3 74.9 reduce-scatter.2

commit v3 on v2

--- a/solution.py
+++ b/solution.py
@@ -374,54 +374,58 @@
     ).reshape(-1)
     from_root = jnp.concatenate([root_block, off_one], 1)
     from_second = jnp.concatenate([turn_one, diag_one], 0)
-    uppers = []
-    lowers = []
-    panels = []
-    slots = []
+    offs = []
+    diags = []
     parent_slots = upper_len + row_at * dev_blocks + jnp.arange(dev_blocks)
     for at in range(bottom_dev):
+        last = at + 1 == bottom_dev
         listed = bottom_lists[at, :upper_len]
         matches = listed[:, None] == upper_blocks[None, :]
         member_rows = jnp.repeat(jnp.any(matches, axis=0), block_rows)
         upper_slots = jnp.sum(jnp.where(matches, jnp.arange(upper_len)[:, None], 0), axis=0)
-        slots.append(jnp.concatenate([upper_slots, parent_slots]).astype(jnp.int32))
+        slots = jnp.concatenate([upper_slots, parent_slots]).astype(jnp.int32)
         width_three = node_width(widths, NODES - BOTTOM + bottom_dev * group_at + at)
         keep_three = own_index < width_three
-        keep_upper = member_rows[:, None] & keep_three[None, :]
-        panel = lax.all_gather(bottom_panels[at], "row", axis=0, tiled=True)
-        top, low = panel[:upper_rows], panel[upper_rows:]
         listed_root = pick_columns(from_root, listed, block_rows)
         listed_second = pick_rows(from_second, listed, block_rows)
         listed_parent = pick_rows(turn_two, listed, block_rows)
-        product_root = product(listed_root, top) + product(full_root, low)
-        product_second = inner(listed_second, top) + product(full_second, low)
-        upper = jnp.concatenate([product_root, product_second], 0)
-        lower = inner(listed_parent, top) + inner(diag_full, low)
-        uppers.append(jnp.where(keep_upper, -upper, 0).astype(jnp.bfloat16))
-        lowers.append(jnp.where(keep_three[None, :], -lower, 0).astype(jnp.bfloat16))
-        panels.append(panel)
-    fulls = []
-    for at in range(bottom_dev):
-        mine = jnp.concatenate([uppers[at], lowers[at]], 0)
-        other = jnp.concatenate([swap_columns(uppers[at]), swap_columns(lowers[at])], 0)
-        fulls.append(beside(mine, other, col_at, 1))
-    diags = []
-    for at in range(bottom_dev):
-        width_three = node_width(widths, NODES - BOTTOM + bottom_dev * group_at + at)
-        mask_three = (own_index < width_three)[:, None] & (row_index < width_three)[None, :]
-        term = inner(fulls[at], pick_rows(panels[at], slots[at], block_rows))
-        summed = lax.psum_scatter(
-            term.astype(jnp.bfloat16), "row", scatter_dimension=0, tiled=True
-        ).astype(jnp.float32).T
+        edges = [0, own_cols * 3 // 4, own_cols] if last else [0, own_cols]
+        mine = []
+        other = []
+        kept = []
+        for low_edge, high_edge in zip(edges, edges[1:]):
+            keep_piece = keep_three[low_edge:high_edge][None, :]
+            panel = lax.all_gather(
+                bottom_panels[at, :, low_edge:high_edge], "row", axis=0, tiled=True
+            )
+            top, low = panel[:upper_rows], panel[upper_rows:]
+            product_root = product(listed_root, top) + product(full_root, low)
+            product_second = inner(listed_second, top) + product(full_second, low)
+            upper = jnp.concatenate([product_root, product_second], 0)
+            lower = inner(listed_parent, top) + inner(diag_full, low)
+            upper = jnp.where(member_rows[:, None] & keep_piece, -upper, 0).astype(jnp.bfloat16)
+            lower = jnp.where(keep_piece, -lower, 0).astype(jnp.bfloat16)
+            other_upper = swap_columns(upper)
+            other_lower = swap_columns(lower)
+            mine.append(jnp.concatenate([upper, lower], 0))
+            other.append(jnp.concatenate([other_upper, other_lower], 0))
+            kept.append(pick_rows(panel, slots, block_rows))
+        offs.append(jnp.concatenate(mine, 1).reshape(3, rows_dev, own_cols))
+        kept = lax.optimization_barrier(jnp.concatenate(kept, 1))
+        terms = [
+            jnp.concatenate([inner(part, kept).astype(jnp.bfloat16) for part in parts], 0)
+            for parts in (mine, other)
+        ]
+        term = beside(*terms, col_at, 0)
+        summed = lax.psum_scatter(term, "row", scatter_dimension=0, tiled=True)
+        mask_three = keep_three[:, None] & (row_index < width_three)[None, :]
         diags.append(
-            jnp.where(mask_three, bottom_inverse[at].astype(jnp.float32) - summed, 0).astype(
-                jnp.bfloat16
-            )
+            jnp.where(
+                mask_three,
+                bottom_inverse[at].astype(jnp.float32) - summed.astype(jnp.float32).T,
+                0,
+            ).astype(jnp.bfloat16)
         )
-    offs = [
-        jnp.concatenate([upper, lower], 0).reshape(3, rows_dev, own_cols)
-        for upper, lower in zip(uppers, lowers)
-    ]
     return (
         second_off,
         second_diag,

time: 755 us -> 864 us (1.14)
  waiting for transfers between devices: 342 us -> 487 us
  starting transfers between devices: 76.3 us -> 53.3 us
  matrix products: 138 us -> 117 us
  other arithmetic: 48.3 us -> 66.5 us
  local copies, waits for them, and re-layouts: 48.5 us -> 32.9 us
    all_gather x1, waiting for transfers between devices: 0.02 us -> 53.7 us  [local_paired(): panel_two = lax.all_gather(third_panels[0], 'row', axis=1, tiled=True)]
    reduce_scatter x2, waiting for transfers between devices: 48.3 us -> 83.3 us  [local_paired(): summed = lax.psum_scatter(term, 'row', scatter_dimension=0, tiled=True)]
    ppermute x6, starting transfers between devices: 50.6 us -> 24.9 us  [row_exchange(): came = lax.ppermute(sent, 'row', row_route(apart))]
    ppermute x14 -> x16, waiting for transfers between devices: 112 us -> 135 us  [swap_columns(): return lax.ppermute(block, 'col', [(0, 1), (1, 0)])]
    all_gather x2 -> x3, waiting for transfers between devices: 57.4 us -> 76.3 us  [local_paired(): lax.all_gather(bottom_panels[at, :, low_edge:high_edge], 'row', axis=0, t...]
    ppermute x6, waiting for transfers between devices: 65.5 us -> 81.2 us  [row_exchange(): came = lax.ppermute(sent, 'row', row_route(apart))]
    dot_general x12 -> x19, matrix products: 90.8 us -> 75.6 us  [inner(): lax.dot_general(left, right, (((0,), (0,)), ((), ())), preferred_element_...]
    concatenate x3 -> x4, other arithmetic: 4.35 us -> 14.3 us  [the longest x1 9.3 us: local_paired(): offs.append(jnp.concatenate(mine, 1).reshape(3, rows_dev, own_cols))]
  transfers between devices with their start and end apart: 31 -> 34, of which waited for: 22 -> 17; matrix products, arithmetic and copies ran while one was open for 30% -> 24% of each run, Pallas kernels for 11% -> 10%
where the time goes in v3:
time: 864 us; the launch traced here: 858 us
  waiting for transfers between devices  487 us (56%)
  matrix products  117 us (14%)
  Pallas kernels  86.7 us (10%)
  other arithmetic  66.5 us (8%)
  starting transfers between devices  53.3 us (6%)
  local copies, waits for them, and re-layouts  32.9 us (4%)
  between operations  15.5 us (2%)
    ppermute x16, waiting for transfers between devices, swap_columns(): return lax.ppermute(block, 'col', [(0, 1), (1, 0)])  135 us
    reduce_scatter x2, waiting for transfers between devices, local_paired(): summed = lax.psum_scatter(term, 'row', scatter_dimension=0, tiled=True)  83.3 us
    ppermute x6, waiting for transfers between devices, row_exchange(): came = lax.ppermute(sent, 'row', row_route(apart))  81.2 us
    all_gather x3, waiting for transfers between devices, local_paired(): lax.all_gather(bottom_panels[at, :, low_edge:high_edge], 'row', axis=0, t...  76.3 us
    dot_general x19, matrix products, inner(): lax.dot_general(left, right, (((0,), (0,)), ((), ())), preferred_element_...  75.6 us
    pallas_call x7, Pallas kernels, pick_rows(): pl.pallas_call(copy_block, out_shape=jax.ShapeDtypeStruct((count * height...  66.1 us
    ppermute x3, waiting for transfers between devices, local_paired(): came = lax.ppermute(came, 'row', row_route(apart))  56.7 us
    all_gather x1, waiting for transfers between devices, local_paired(): panel_two = lax.all_gather(third_panels[0], 'row', axis=1, tiled=True)  53.7 us
  transfers between devices with their start and end apart: 34, of which 17 were waited for; matrix products, arithmetic and copies ran while one was open for 24% of the time, Pallas kernels for 10%

profile of v3, /device:TPU:0, one launch (start us, length us, event | category | flops | bytes accessed | tf_op | source)
XLA Modules:
  0.0 858.3 jit_solution(6567768547040328961)
XLA Ops:
  9.9 2.7 slice.59
  12.7 3.1 collective-permute-start
  15.9 2.6 collective-permute-start.1
  20.4 34.1 %collective-permute-done = bf16[512,512]{1,0:T(8,128)(2,1)S(1)} collective-permute-done((bf16[512,512]{1,0:T(8,128)(2,1)S(1)}, bf16[512,512]{1,0:T(8,128)(2,1)S(1)}, u32[]{:S(2)}, u32[]{:S(2)}) %collective-permute-start) | collective-permute-done | bytes 524320 | tf_op jit(solution)/shard_map/ppermute | solution.py:307
  56.6 5.4 collective-permute-done.1
  63.6 17.3 %collective-permute-done.2 = bf16[512,512]{1,0:T(8,128)(2,1)S(1)} collective-permute-done((bf16[512,512]{1,0:T(8,128)(2,1)S(1)}, bf16[512,512]{1,0:T(8,128)(2,1)S(1)}, u32[]{:S(2)}, u32[]{:S(2)}) %collective-permute-start.2) | collective-permute-done | bytes 524320 | tf_op jit(solution)/shard_map/ppermute | solution.py:307
  82.9 8.5 collective-permute-done.6
  91.5 2.8 maximum_select_fusion.1
  103.0 11.1 %select_convert_fusion.1 = bf16[512,2048]{1,0:T(8,128)(2,1)S(1)} fusion(bf16[512,2048]{1,0:T(8,128)(2,1)S(1)} %and_select_fusion, pred[2048]{0:T(1024)(128)(4,1)S(1)} %iota_compare_fusion.1, bf16[2048,1024]{1,0:T(8,128)(2,1)} %collective-permute-done.7, bf16[2048,1024]{1,0:T(8,128)(2,1)} %maximum_select_fusion.1, pred[]{:T(512)S(6)} %eq.78), kind=kOutput, calls=%fused_computation.16 | convolution fusion | flops 4335861760 | bytes 12584961 | tf_op jit(solution)/shard_map/dot_general | solution.py:264
  115.6 18.4 %collective-permute-start.10 = (bf16[128,512]{1,0:T(8,128)(2,1)S(1)}, bf16[128,512]{1,0:T(8,128)(2,1)S(1)}, u32[]{:S(2)}, u32[]{:S(2)}) collective-permute-start(bf16[128,512]{1,0:T(8,128)(2,1)S(1)} %get-tuple-element.38), channel_id=1, source_target_pairs={{0,2},{2,0},{4,6},{6,4},{1,3},{3,1},{5,7},{7,5},{8,10},{10,8},{12,... | collective-permute-start | bytes 393224 | tf_op jit(solution)/shard_map/ppermute | solution.py:258
  139.4 6.0 collective-permute-done.10
  145.4 3.3 collective-permute-done.11
  148.7 6.9 collective-permute-done.12
  158.0 11.0 %collective-permute-done.13 = bf16[4,128,512]{2,1,0:T(8,128)(2,1)S(1)} collective-permute-done((bf16[4,128,512]{2,1,0:T(8,128)(2,1)S(1)}, bf16[4,128,512]{2,1,0:T(8,128)(2,1)S(1)}, u32[]{:S(2)}, u32[]{:S(2)}) %collective-permute-start.13) | collective-permute-done | bytes 524320 | tf_op jit(solution)/shard_map/ppermute | solution.py:239
  170.3 2.8 maximum_select_fusion.12
  177.1 7.4 pick_rows.13
  184.5 3.5 maximum_select_fusion.6
  188.1 17.3 %select_convert_fusion = bf16[2048,512]{1,0:T(8,128)(2,1)} fusion(bf16[1024,512]{1,0:T(8,128)(2,1)} %collective-permute-done.9, bf16[1024,512]{1,0:T(8,128)(2,1)} %maximum_select_fusion.12, pred[]{:T(512)S(6)} %eq.78, pred[512]{0:T(512)(128)(4,1)S(1)} %fusion.83, pred[2048]{0:T(1024)(128)(4,1)S(1)} %iota_compare_fusion.1, bf16[2048,512]{1,0:T(8,128)(2,1)} %bitcast.186, ...), kind=kOutput, calls=%fused_computation.15 | convolution fusion | flops 4347396096 | bytes 14682625 | tf_op jit(solution)/shard_map/dot_general | solution.py:268
  205.4 53.7 %all-gather.9.cloned.1.call-done = bf16[1,2,2048,1024]{3,2,1,0:T(8,128)(2,1)} async-done(((bf16[1,2,512,1024]{3,2,1,0:T(8,128)(2,1)}), bf16[1,2,2048,1024]{3,2,1,0:T(8,128)(2,1)}) %all-gather.9.cloned.1.call-update) | async-done | bytes 8388624 | tf_op jit(solution)/shard_map/all_gather | solution.py:334
  259.1 4.7 fusion.3
  264.4 2.4 fusion.4
  266.8 2.3 fusion.52
  274.8 2.5 pad_maximum_fusion.1.blocks_in
  277.2 10.3 %pick_columns.3 = bf16[512,2048]{1,0:T(8,128)(2,1)} custom-call(s32[16]{0:T(128)} %copy-done.39, bf16[512,4096]{1,0:T(8,128)(2,1)} %pad_maximum_fusion.1.blocks_in), custom_call_target="tpu_custom_call" | custom-call | bytes 4194304 | tf_op jit(solution)/shard_map/pick_columns/pallas_call | solution.py:195
  287.5 3.3 fusion.65
  293.1 10.2 %pick_rows.9 = bf16[2048,512]{1,0:T(8,128)(2,1)} custom-call(s32[16]{0:T(128)} %copy-done.39, bf16[4096,512]{1,0:T(8,128)(2,1)} %pad_maximum_fusion.2.blocks_in), custom_call_target="tpu_custom_call" | custom-call | bytes 4194304 | tf_op jit(solution)/shard_map/pick_rows/pallas_call | solution.py:214
  306.8 76.3 %all-gather.13.cloned.1.call-done = bf16[1,4096,768]{2,1,0:T(8,128)(2,1)} async-done(((bf16[1,1024,768]{2,1,0:T(8,128)(2,1)}), bf16[1,4096,768]{2,1,0:T(8,128)(2,1)}) %all-gather.13.cloned.1.call-update) | async-done | bytes 6291472 | tf_op jit(solution)/shard_map/all_gather | solution.py:398
  383.1 5.5 fusion.20
  388.6 8.7 %pick_rows.12 = bf16[1536,768]{1,0:T(8,128)(2,1)} custom-call(s32[12]{0:T(128)} %get-tuple-element.42.picks, bf16[4096,768]{1,0:T(8,128)(2,1)} %bitcast.178), custom_call_target="tpu_custom_call" | custom-call | bytes 4718592 | tf_op jit(solution)/shard_map/pick_rows/pallas_call | solution.py:214
  398.8 2.8 collective-permute-start.17
  401.6 4.0 pad_maximum_fusion.4
  407.1 64.9 %collective-permute-done.17 = bf16[512,512]{1,0:T(8,128)(2,1)S(1)} collective-permute-done((bf16[512,512]{1,0:T(8,128)(2,1)}, bf16[512,512]{1,0:T(8,128)(2,1)S(1)}, u32[]{:S(2)}, u32[]{:S(2)}) %collective-permute-start.17) | collective-permute-done | bytes 524320 | tf_op jit(solution)/shard_map/ppermute | solution.py:258
  473.7 3.8 broadcast_select_fusion.1
  486.1 34.6 %collective-permute-done.19 = bf16[2048,512]{1,0:T(8,128)(2,1)S(1)} collective-permute-done((bf16[2048,512]{1,0:T(8,128)(2,1)S(1)}, bf16[2048,512]{1,0:T(8,128)(2,1)S(1)}, u32[]{:S(2)}, u32[]{:S(2)}) %collective-permute-start.19) | collective-permute-done | bytes 2097184 | tf_op jit(solution)/shard_map/ppermute | solution.py:239
  522.1 5.6 fusion.38
  532.3 10.7 %pick_rows.10 = bf16[2048,512]{1,0:T(8,128)(2,1)} custom-call(s32[16]{0:T(128)} %copy-done.39, bf16[4096,512]{1,0:T(8,128)(2,1)} %copy-done), custom_call_target="tpu_custom_call" | custom-call | bytes 4194304 | tf_op jit(solution)/shard_map/pick_rows/pallas_call | solution.py:214
  543.0 34.0 %collective-permute-done.21 = bf16[1024,512]{0,1:T(8,128)(2,1)} collective-permute-done((bf16[1024,512]{0,1:T(8,128)(2,1)}, bf16[1024,512]{0,1:T(8,128)(2,1)}, u32[]{:S(2)}, u32[]{:S(2)}) %collective-permute-start.21) | collective-permute-done | bytes 1048608 | tf_op jit(solution)/shard_map/ppermute | solution.py:239
  577.0 5.0 fusion.21
  585.5 3.0 fusion.67
  588.5 4.1 fusion.45
  595.5 14.3 %collective-permute-done.27 = bf16[512,256]{1,0:T(8,128)(2,1)S(1)} collective-permute-done((bf16[512,256]{1,0:T(8,128)(2,1)S(1)}, bf16[512,256]{1,0:T(8,128)(2,1)S(1)}, u32[]{:S(2)}, u32[]{:S(2)}) %collective-permute-start.27) | collective-permute-done | bytes 262176 | tf_op jit(solution)/shard_map/ppermute | solution.py:239
  610.9 4.1 fusion.42
  615.0 3.8 maximum_select_fusion.4
  619.7 10.3 %pick_columns.2 = bf16[512,2048]{1,0:T(8,128)(2,1)} custom-call(s32[16]{0:T(128)} %copy-done.38, bf16[512,4096]{1,0:T(8,128)(2,1)} %pad_maximum_fusion.1.blocks_in), custom_call_target="tpu_custom_call" | custom-call | bytes 4194304 | tf_op jit(solution)/shard_map/pick_columns/pallas_call | solution.py:195
  630.0 10.3 %pick_rows.7 = bf16[2048,512]{1,0:T(8,128)(2,1)} custom-call(s32[16]{0:T(128)} %copy-done.38, bf16[4096,512]{1,0:T(8,128)(2,1)} %pad_maximum_fusion.2.blocks_in), custom_call_target="tpu_custom_call" | custom-call | bytes 4194304 | tf_op jit(solution)/shard_map/pick_rows/pallas_call | solution.py:214
  640.3 4.7 fusion.8
  647.9 2.3 fusion.48
  650.3 2.4 fusion.100
  654.8 10.2 %pick_rows.8 = bf16[2048,512]{1,0:T(8,128)(2,1)} custom-call(s32[16]{0:T(128)} %copy-done.38, bf16[4096,512]{1,0:T(8,128)(2,1)} %copy-done), custom_call_target="tpu_custom_call" | custom-call | bytes 4194304 | tf_op jit(solution)/shard_map/pick_rows/pallas_call | solution.py:214
  665.1 5.9 fusion.9
  671.0 4.6 select_convert_fusion.2
  676.2 8.7 %pick_rows.11 = bf16[1536,1024]{1,0:T(8,128)(2,1)} custom-call(s32[12]{0:T(128)} %get-tuple-element.41.picks, bf16[4096,1024]{1,0:T(8,128)(2,1)} %bitcast.185), custom_call_target="tpu_custom_call" | custom-call | bytes 6291456 | tf_op jit(solution)/shard_map/pick_rows/pallas_call | solution.py:214
  684.9 5.9 convolution_convert_fusion
  690.8 11.2 %collective-permute-done.22 = bf16[1024,1024]{1,0:T(8,128)(2,1)} collective-permute-done((bf16[1024,1024]{1,0:T(8,128)(2,1)S(1)}, bf16[1024,1024]{1,0:T(8,128)(2,1)}, u32[]{:S(2)}, u32[]{:S(2)}) %collective-permute-start.22) | collective-permute-done | bytes 2097184 | tf_op jit(solution)/shard_map/ppermute | solution.py:239
  702.0 20.9 %collective-permute-done.23 = bf16[512,1024]{1,0:T(8,128)(2,1)} collective-permute-done((bf16[512,1024]{1,0:T(8,128)(2,1)S(1)}, bf16[512,1024]{1,0:T(8,128)(2,1)}, u32[]{:S(2)}, u32[]{:S(2)}) %collective-permute-start.23) | collective-permute-done | bytes 1048608 | tf_op jit(solution)/shard_map/ppermute | solution.py:239
  722.9 5.6 fusion.39
  728.5 3.8 maximum_select_fusion.3
  732.3 2.7 fusion.97
  736.4 2.4 copy.26
  745.5 2.4 copy.23
  749.1 9.3 %maximum_maximum_fusion = bf16[1536,1024]{1,0:T(8,128)(2,1)S(1)} fusion(bf16[512,256]{1,0:T(8,128)(2,1)S(1)} %fusion.55, bf16[1024,256]{1,0:T(8,128)(2,1)S(1)} %copy-done.23, bf16[512,768]{1,0:T(8,128)(2,1)S(1)} %copy-done.35, bf16[1024,768]{1,0:T(8,128)(2,1)} %fusion.13), kind=kLoop, calls=%fused_computation.34 | loop fusion | flops 12582912 | bytes 6291456 | tf_op jit(solution)/shard_map/concatenate | solution.py:413
  758.4 3.2 pad_maximum_fusion
  763.5 83.3 %reduce-scatter.3.cloned.1.call-done = bf16[512,1024]{1,0:T(8,128)(2,1)} async-done(((bf16[2048,1024]{1,0:T(8,128)(2,1)}), bf16[512,1024]{1,0:T(8,128)(2,1)}) %reduce-scatter.3.cloned.1.call-update) | async-done | bytes 1048592 | tf_op jit(solution)/shard_map/reduce_scatter | solution.py:420
  848.6 2.6 copy.24
  (233 shorter events, 91.3 us)
Async XLA Ops:
  7.2 169.9 %all-gather.15.cloned.1.call-start = ((), (), s32[]{:S(2)}) async-start(), calls=%async_computation.7 | async-start | bytes 2621440 | tf_op jit(solution)/shard_map/all_gather | solution.py:398
  9.1 250.0 %all-gather.9.cloned.1.call-start = ((), (), s32[]{:S(2)}) async-start(), calls=%async_computation.4 | async-start | bytes 10485760 | tf_op jit(solution)/shard_map/all_gather | solution.py:334
  9.9 373.2 %all-gather.13.cloned.1.call-start = ((), (), s32[]{:S(2)}) async-start(), calls=%async_computation.6 | async-start | bytes 7864320 | tf_op jit(solution)/shard_map/all_gather | solution.py:398
  12.7 627.6 %all-gather.11.cloned.1.call-start = ((), (), s32[]{:S(2)}) async-start(), calls=%async_computation.5 | async-start | bytes 10485760 | tf_op jit(solution)/shard_map/all_gather | solution.py:398
  12.7 41.7 %collective-permute-start = (bf16[512,512]{1,0:T(8,128)(2,1)S(1)}, bf16[512,512]{1,0:T(8,128)(2,1)S(1)}, u32[]{:S(2)}, u32[]{:S(2)}) collective-permute-start(bf16[512,512]{1,0:T(8,128)(2,1)S(1)} %bitcast.194), channel_id=1, source_target_pairs={{0,2},{2,0},{4,6},{6,4},{1,3},{3,1},{5,7},{7,5},{8,10},{10,8},{12,... | collective-permute-start | bytes 1572872 | tf_op jit(solution)/shard_map/ppermute | solution.py:307
  15.9 46.1 %collective-permute-start.1 = (bf16[512,512]{1,0:T(8,128)(2,1)S(1)}, bf16[512,512]{1,0:T(8,128)(2,1)S(1)}, u32[]{:S(2)}, u32[]{:S(2)}) collective-permute-start(bf16[512,512]{1,0:T(8,128)(2,1)S(1)} %bitcast.195), channel_id=1, source_target_pairs={{0,4},{2,6},{4,0},{6,2},{1,5},{3,7},{5,1},{7,3},{8,12},{10,14},{12... | collective-permute-start | bytes 1572872 | tf_op jit(solution)/shard_map/ppermute | solution.py:307
  18.4 62.4 %collective-permute-start.2 = (bf16[512,512]{1,0:T(8,128)(2,1)S(1)}, bf16[512,512]{1,0:T(8,128)(2,1)S(1)}, u32[]{:S(2)}, u32[]{:S(2)}) collective-permute-start(bf16[512,512]{1,0:T(8,128)(2,1)S(1)} %bitcast.196), channel_id=1, source_target_pairs={{0,6},{2,4},{4,2},{6,0},{1,7},{3,5},{5,3},{7,1},{8,14},{10,12},{12... | collective-permute-start | bytes 1572872 | tf_op jit(solution)/shard_map/ppermute | solution.py:307
  18.4 64.0 %collective-permute-start.3 = (bf16[512,512]{1,0:T(8,128)(2,1)S(1)}, bf16[512,512]{1,0:T(8,128)(2,1)S(1)}, u32[]{:S(2)}, u32[]{:S(2)}) collective-permute-start(bf16[512,512]{1,0:T(8,128)(2,1)S(1)} %bitcast.197), channel_id=1, source_target_pairs={{0,1},{1,0},{2,3},{3,2},{4,5},{5,4},{6,7},{7,6},{8,9},{9,8},{10,11... | collective-permute-start | bytes 1572872 | tf_op jit(solution)/shard_map/ppermute | solution.py:239
  54.5 28.3 %collective-permute-start.4 = (bf16[512,512]{1,0:T(8,128)(2,1)S(1)}, bf16[512,512]{1,0:T(8,128)(2,1)S(1)}, u32[]{:S(2)}, u32[]{:S(2)}) collective-permute-start(bf16[512,512]{1,0:T(8,128)(2,1)S(1)} %collective-permute-done), channel_id=1, source_target_pairs={{0,1},{1,0},{2,3},{3,2},{4,5},{5,4},{6,7},{7,6},{8,9},{9,8},{10,11... | collective-permute-start | bytes 1572872 | tf_op jit(solution)/shard_map/ppermute | solution.py:239
  62.0 20.9 %collective-permute-start.5 = (bf16[512,512]{1,0:T(8,128)(2,1)S(1)}, bf16[512,512]{1,0:T(8,128)(2,1)S(1)}, u32[]{:S(2)}, u32[]{:S(2)}) collective-permute-start(bf16[512,512]{1,0:T(8,128)(2,1)S(1)} %collective-permute-done.1), channel_id=1, source_target_pairs={{0,1},{1,0},{2,3},{3,2},{4,5},{5,4},{6,7},{7,6},{8,9},{9,8},{10,11... | collective-permute-start | bytes 1572872 | tf_op jit(solution)/shard_map/ppermute | solution.py:239
  80.9 10.5 %collective-permute-start.6 = (bf16[512,512]{1,0:T(8,128)(2,1)S(1)}, bf16[512,512]{1,0:T(8,128)(2,1)S(1)}, u32[]{:S(2)}, u32[]{:S(2)}) collective-permute-start(bf16[512,512]{1,0:T(8,128)(2,1)S(1)} %collective-permute-done.2), channel_id=1, source_target_pairs={{0,1},{1,0},{2,3},{3,2},{4,5},{5,4},{6,7},{7,6},{8,9},{9,8},{10,11... | collective-permute-start | bytes 1572872 | tf_op jit(solution)/shard_map/ppermute | solution.py:239
  94.2 8.7 %collective-permute-start.7 = (bf16[2048,1024]{1,0:T(8,128)(2,1)}, bf16[2048,1024]{1,0:T(8,128)(2,1)}, u32[]{:S(2)}, u32[]{:S(2)}) collective-permute-start(bf16[2048,1024]{1,0:T(8,128)(2,1)} %maximum_select_fusion.1), channel_id=1, source_target_pairs={{0,8},{8,0},{16,24},{24,16},{1,9},{9,1},{17,25},{25,17},{2,10},{10... | collective-permute-start | bytes 12582920 | tf_op jit(solution)/shard_map/ppermute | solution.py:19
  94.2 76.0 %collective-permute-start.8 = (bf16[512,512]{1,0:T(8,128)(2,1)}, bf16[512,512]{1,0:T(8,128)(2,1)}, u32[]{:S(2)}, u32[]{:S(2)}) collective-permute-start(bf16[512,512]{1,0:T(8,128)(2,1)} %bitcast.11), channel_id=1, source_target_pairs={{0,1},{1,0},{2,3},{3,2},{4,5},{5,4},{6,7},{7,6},{8,9},{9,8},{10,11... | collective-permute-start | bytes 1572872 | tf_op jit(solution)/shard_map/ppermute | solution.py:239
  97.3 664.4 %reduce-scatter.5.cloned.1.call-start = ((), (), s32[]{:S(2)}) async-start(), calls=%async_computation.3 | async-start | bytes 5242880 | tf_op jit(solution)/shard_map/reduce_scatter | solution.py:420
  115.6 29.8 %collective-permute-start.10 = (bf16[128,512]{1,0:T(8,128)(2,1)S(1)}, bf16[128,512]{1,0:T(8,128)(2,1)S(1)}, u32[]{:S(2)}, u32[]{:S(2)}) collective-permute-start(bf16[128,512]{1,0:T(8,128)(2,1)S(1)} %get-tuple-element.38), channel_id=1, source_target_pairs={{0,2},{2,0},{4,6},{6,4},{1,3},{3,1},{5,7},{7,5},{8,10},{10,8},{12,... | collective-permute-start | bytes 393224 | tf_op jit(solution)/shard_map/ppermute | solution.py:258
  134.8 14.0 %collective-permute-start.11 = (bf16[128,512]{1,0:T(8,128)(2,1)S(1)}, bf16[128,512]{1,0:T(8,128)(2,1)S(1)}, u32[]{:S(2)}, u32[]{:S(2)}) collective-permute-start(bf16[128,512]{1,0:T(8,128)(2,1)S(1)} %get-tuple-element.37), channel_id=1, source_target_pairs={{0,4},{2,6},{4,0},{6,2},{1,5},{3,7},{5,1},{7,3},{8,12},{10,14},{12... | collective-permute-start | bytes 393224 | tf_op jit(solution)/shard_map/ppermute | solution.py:258
  136.7 18.9 %collective-permute-start.12 = (bf16[128,512]{1,0:T(8,128)(2,1)S(1)}, bf16[128,512]{1,0:T(8,128)(2,1)S(1)}, u32[]{:S(2)}, u32[]{:S(2)}) collective-permute-start(bf16[128,512]{1,0:T(8,128)(2,1)S(1)} %get-tuple-element.36), channel_id=1, source_target_pairs={{0,6},{2,4},{4,2},{6,0},{1,7},{3,5},{5,3},{7,1},{8,14},{10,12},{12... | collective-permute-start | bytes 393224 | tf_op jit(solution)/shard_map/ppermute | solution.py:258
  155.7 13.4 %collective-permute-start.13 = (bf16[4,128,512]{2,1,0:T(8,128)(2,1)S(1)}, bf16[4,128,512]{2,1,0:T(8,128)(2,1)S(1)}, u32[]{:S(2)}, u32[]{:S(2)}) collective-permute-start(bf16[4,128,512]{2,1,0:T(8,128)(2,1)S(1)} %bitcast_dynamic-update-slice_fusion.11), channel_id=1, source_target_pairs={{0,1},{1,0},{2,3},{3,2},{4,5},{5,4},{6,7},{7,6},{8,9},{9,8},{10,11... | collective-permute-start | bytes 1572872 | tf_op jit(solution)/shard_map/ppermute | solution.py:239
  169.5 15.1 %collective-permute-start.14 = (bf16[4,256,512]{2,1,0:T(8,128)(2,1)S(1)}, bf16[4,256,512]{2,1,0:T(8,128)(2,1)}, u32[]{:S(2)}, u32[]{:S(2)}) collective-permute-start(bf16[4,256,512]{2,1,0:T(8,128)(2,1)S(1)} %maximum_select_fusion.13), channel_id=1, source_target_pairs={{0,8},{8,0},{16,24},{24,16},{1,9},{9,1},{17,25},{25,17},{2,10},{10... | collective-permute-start | bytes 3145736 | tf_op jit(solution)/shard_map/ppermute | solution.py:19
  170.2 5.7 copy-start.40
  173.1 15.0 %collective-permute-start.9 = (bf16[1024,512]{1,0:T(8,128)(2,1)}, bf16[1024,512]{1,0:T(8,128)(2,1)}, u32[]{:S(2)}, u32[]{:S(2)}) collective-permute-start(bf16[1024,512]{1,0:T(8,128)(2,1)} %maximum_select_fusion.12), channel_id=1, source_target_pairs={{0,8},{8,0},{16,24},{24,16},{1,9},{9,1},{17,25},{25,17},{2,10},{10... | collective-permute-start | bytes 3145736 | tf_op jit(solution)/shard_map/ppermute | solution.py:19
  176.0 12.1 %copy-start.38 = (s32[16]{0:T(128)}, s32[16]{0:T(128)S(1)}, u32[]{:S(2)}) copy-start(s32[16]{0:T(128)S(1)} %get-tuple-element.39.picks) | copy-start | bytes 196
  176.0 12.1 %copy-start.39 = (s32[16]{0:T(128)}, s32[16]{0:T(128)S(1)}, u32[]{:S(2)}) copy-start(s32[16]{0:T(128)S(1)} %get-tuple-element.40.picks) | copy-start | bytes 196
  259.1 4.7 copy-start.14
  259.1 5.3 copy-start.42
  273.3 30.0 %collective-permute-start.15 = (bf16[512,1024]{1,0:T(8,128)(2,1)}, bf16[512,1024]{1,0:T(8,128)(2,1)}, u32[]{:S(2)}, u32[]{:S(2)}) collective-permute-start(bf16[512,1024]{1,0:T(8,128)(2,1)} %get-tuple-element.35), channel_id=1, source_target_pairs={{0,1},{1,0},{2,3},{3,2},{4,5},{5,4},{6,7},{7,6},{8,9},{9,8},{10,11... | collective-permute-start | bytes 3145736 | tf_op jit(solution)/shard_map/ppermute | solution.py:239
  277.2 10.3 %copy-start.24 = (bf16[1,4096,256]{2,1,0:T(8,128)(2,1)S(1)}, bf16[1,4096,256]{2,1,0:T(8,128)(2,1)}, u32[]{:S(2)}) copy-start(bf16[1,4096,256]{2,1,0:T(8,128)(2,1)} %all-gather.15.cloned.1.call-done) | copy-start | bytes 6291460
  306.8 99.1 %collective-permute-start.16 = (bf16[512,512]{1,0:T(8,128)(2,1)}, bf16[512,512]{1,0:T(8,128)(2,1)}, u32[]{:S(2)}, u32[]{:S(2)}) collective-permute-start(bf16[512,512]{1,0:T(8,128)(2,1)} %get-tuple-element.33), channel_id=1, source_target_pairs={{0,2},{2,0},{4,6},{6,4},{1,3},{3,1},{5,7},{7,5},{8,10},{10,8},{12,... | collective-permute-start | bytes 1572872 | tf_op jit(solution)/shard_map/ppermute | solution.py:258
  397.2 76.4 %collective-permute-start.20 = (bf16[512,1024]{1,0:T(8,128)(2,1)S(1)}, bf16[512,1024]{1,0:T(8,128)(2,1)S(1)}, u32[]{:S(2)}, u32[]{:S(2)}) collective-permute-start(bf16[512,1024]{1,0:T(8,128)(2,1)S(1)} %get-tuple-element.34), channel_id=1, source_target_pairs={{0,1},{1,0},{2,3},{3,2},{4,5},{5,4},{6,7},{7,6},{8,9},{9,8},{10,11... | collective-permute-start | bytes 3145736 | tf_op jit(solution)/shard_map/ppermute | solution.py:239
  398.8 6.8 copy-start.36
  398.8 73.3 %collective-permute-start.17 = (bf16[512,512]{1,0:T(8,128)(2,1)}, bf16[512,512]{1,0:T(8,128)(2,1)S(1)}, u32[]{:S(2)}, u32[]{:S(2)}) collective-permute-start(bf16[512,512]{1,0:T(8,128)(2,1)} %get-tuple-element.32), channel_id=1, source_target_pairs={{0,4},{2,6},{4,0},{6,2},{1,5},{3,7},{5,1},{7,3},{8,12},{10,14},{12... | collective-permute-start | bytes 1572872 | tf_op jit(solution)/shard_map/ppermute | solution.py:258
  405.6 66.5 %collective-permute-start.18 = (bf16[512,512]{1,0:T(8,128)(2,1)S(1)}, bf16[512,512]{1,0:T(8,128)(2,1)S(1)}, u32[]{:S(2)}, u32[]{:S(2)}) collective-permute-start(bf16[512,512]{1,0:T(8,128)(2,1)S(1)} %copy-done.36), channel_id=1, source_target_pairs={{0,6},{2,4},{4,2},{6,0},{1,7},{3,5},{5,3},{7,1},{8,14},{10,12},{12... | collective-permute-start | bytes 1572872 | tf_op jit(solution)/shard_map/ppermute | solution.py:258
  405.9 71.6 %slice-start = ((s8[6291456]{0:T(1024)(128)(4,1)}), s8[4194304]{0:T(1024)(128)(4,1)S(1)}, s32[]{:S(2)}) async-start(s8[6291456]{0:T(1024)(128)(4,1)} %bitcast.179), calls=%async_computation.8 | async-start | bytes 8388608
  472.1 5.3 slice-start.1
  472.1 48.6 %collective-permute-start.19 = (bf16[2048,512]{1,0:T(8,128)(2,1)S(1)}, bf16[2048,512]{1,0:T(8,128)(2,1)S(1)}, u32[]{:S(2)}, u32[]{:S(2)}) collective-permute-start(bf16[2048,512]{1,0:T(8,128)(2,1)S(1)} %bitcast.189), channel_id=1, source_target_pairs={{0,1},{1,0},{2,3},{3,2},{4,5},{5,4},{6,7},{7,6},{8,9},{9,8},{10,11... | collective-permute-start | bytes 6291464 | tf_op jit(solution)/shard_map/ppermute | solution.py:239
  477.4 51.7 %copy-start.29 = (bf16[512,2048]{1,0:T(8,128)(2,1)}, bf16[512,2048]{1,0:T(8,128)(2,1)S(1)}, u32[]{:S(2)}) copy-start(bf16[512,2048]{1,0:T(8,128)(2,1)S(1)} %get-tuple-element.28) | copy-start | bytes 6291460
  477.4 52.4 %copy-start.27 = (bf16[512,2048]{1,0:T(8,128)(2,1)}, bf16[512,2048]{1,0:T(8,128)(2,1)S(1)}, u32[]{:S(2)}) copy-start(bf16[512,2048]{1,0:T(8,128)(2,1)S(1)} %get-tuple-element.27) | copy-start | bytes 6291460
  481.9 40.1 %slice-start.4 = ((s8[8388608]{0:T(1024)(128)(4,1)}), s8[4194304]{0:T(1024)(128)(4,1)S(1)}, s32[]{:S(2)}) async-start(s8[8388608]{0:T(1024)(128)(4,1)} %bitcast.200), calls=%async_computation.12 | async-start | bytes 8388608
  483.8 38.3 %slice-start.5 = ((s8[8388608]{0:T(1024)(128)(4,1)}), s8[4194304]{0:T(1024)(128)(4,1)S(1)}, s32[]{:S(2)}) async-start(s8[8388608]{0:T(1024)(128)(4,1)} %bitcast.200), calls=%async_computation.13 | async-start | bytes 8388608
  485.5 36.6 %copy-start.31 = (bf16[1,1024,512]{1,2,0:T(8,128)(2,1)S(1)}, bf16[1,1024,512]{1,2,0:T(8,128)(2,1)}, u32[]{:S(2)}) copy-start(bf16[1,1024,512]{1,2,0:T(8,128)(2,1)} %copy.20) | copy-start | bytes 3145732
  485.5 125.4 %collective-permute-start.24 = (bf16[1024,768]{1,0:T(8,128)(2,1)}, bf16[1024,768]{1,0:T(8,128)(2,1)}, u32[]{:S(2)}, u32[]{:S(2)}) collective-permute-start(bf16[1024,768]{1,0:T(8,128)(2,1)} %fusion.13), channel_id=1, source_target_pairs={{0,1},{1,0},{2,3},{3,2},{4,5},{5,4},{6,7},{7,6},{8,9},{9,8},{10,11... | collective-permute-start | bytes 4718600 | tf_op jit(solution)/shard_map/ppermute | solution.py:239
  522.0 5.7 copy-start
  522.1 7.1 copy-start.25
  527.7 49.3 %collective-permute-start.21 = (bf16[1024,512]{0,1:T(8,128)(2,1)}, bf16[1024,512]{0,1:T(8,128)(2,1)}, u32[]{:S(2)}, u32[]{:S(2)}) collective-permute-start(bf16[1024,512]{0,1:T(8,128)(2,1)} %fusion.38), channel_id=1, source_target_pairs={{0,1},{1,0},{2,3},{3,2},{4,5},{5,4},{6,7},{7,6},{8,9},{9,8},{10,11... | collective-permute-start | bytes 3145736 | tf_op jit(solution)/shard_map/ppermute | solution.py:239
  531.7 62.8 %copy-start.22 = (bf16[1024,256]{1,0:T(8,128)(2,1)}, bf16[1024,256]{1,0:T(8,128)(2,1)S(1)}, u32[]{:S(2)}) copy-start(bf16[1024,256]{1,0:T(8,128)(2,1)S(1)} %fusion.63) | copy-start | bytes 1572868
  531.7 63.8 %collective-permute-start.26 = (bf16[1024,256]{1,0:T(8,128)(2,1)S(1)}, bf16[1024,256]{1,0:T(8,128)(2,1)S(1)}, u32[]{:S(2)}, u32[]{:S(2)}) collective-permute-start(bf16[1024,256]{1,0:T(8,128)(2,1)S(1)} %fusion.63), channel_id=1, source_target_pairs={{0,1},{1,0},{2,3},{3,2},{4,5},{5,4},{6,7},{7,6},{8,9},{9,8},{10,11... | collective-permute-start | bytes 1572872 | tf_op jit(solution)/shard_map/ppermute | solution.py:239
  532.3 49.7 %slice-start.2 = ((s8[6291456]{0:T(1024)(128)(4,1)}), s8[2097152]{0:T(1024)(128)(4,1)S(1)}, s32[]{:S(2)}) async-start(s8[6291456]{0:T(1024)(128)(4,1)} %bitcast.181), calls=%async_computation.10 | async-start | bytes 4194304
  543.0 39.0 %slice-start.3 = ((s8[6291456]{0:T(1024)(128)(4,1)}), s8[4194304]{0:T(1024)(128)(4,1)S(1)}, s32[]{:S(2)}) async-start(s8[6291456]{0:T(1024)(128)(4,1)} %bitcast.181), calls=%async_computation.11 | async-start | bytes 8388608
  543.0 39.0 %copy-start.18 = (bf16[2048,512]{1,0:T(8,128)(2,1)S(1)}, bf16[2048,512]{1,0:T(8,128)(2,1)}, u32[]{:S(2)}) copy-start(bf16[2048,512]{1,0:T(8,128)(2,1)} %pick_rows.10) | copy-start | bytes 6291460
  583.9 4.6 copy-start.34
  584.0 26.9 %collective-permute-start.25 = (bf16[512,768]{1,0:T(8,128)(2,1)S(1)}, bf16[512,768]{1,0:T(8,128)(2,1)S(1)}, u32[]{:S(2)}, u32[]{:S(2)}) collective-permute-start(bf16[512,768]{1,0:T(8,128)(2,1)S(1)} %select_convert_fusion.5), channel_id=1, source_target_pairs={{0,1},{1,0},{2,3},{3,2},{4,5},{5,4},{6,7},{7,6},{8,9},{9,8},{10,11... | collective-permute-start | bytes 2359304 | tf_op jit(solution)/shard_map/ppermute | solution.py:239
  593.4 16.4 %collective-permute-start.27 = (bf16[512,256]{1,0:T(8,128)(2,1)S(1)}, bf16[512,256]{1,0:T(8,128)(2,1)S(1)}, u32[]{:S(2)}, u32[]{:S(2)}) collective-permute-start(bf16[512,256]{1,0:T(8,128)(2,1)S(1)} %fusion.55), channel_id=1, source_target_pairs={{0,1},{1,0},{2,3},{3,2},{4,5},{5,4},{6,7},{7,6},{8,9},{9,8},{10,11... | collective-permute-start | bytes 786440 | tf_op jit(solution)/shard_map/ppermute | solution.py:239
  618.9 227.9 %reduce-scatter.3.cloned.1.call-start = ((), (), s32[]{:S(2)}) async-start(), calls=%async_computation.2 | async-start | bytes 5242880 | tf_op jit(solution)/shard_map/reduce_scatter | solution.py:420
  630.0 10.3 %copy-start.20 = (bf16[512,2048]{1,0:T(8,128)(2,1)S(1)}, bf16[512,2048]{1,0:T(8,128)(2,1)}, u32[]{:S(2)}) copy-start(bf16[512,2048]{1,0:T(8,128)(2,1)} %pick_columns.2) | copy-start | bytes 6291460
  640.3 4.7 copy-start.1
  640.3 5.2 copy-start.30
  653.3 48.7 %collective-permute-start.22 = (bf16[1024,1024]{1,0:T(8,128)(2,1)S(1)}, bf16[1024,1024]{1,0:T(8,128)(2,1)}, u32[]{:S(2)}, u32[]{:S(2)}) collective-permute-start(bf16[1024,1024]{1,0:T(8,128)(2,1)S(1)} %fusion.1), channel_id=1, source_target_pairs={{0,1},{1,0},{2,3},{3,2},{4,5},{5,4},{6,7},{7,6},{8,9},{9,8},{10,11... | collective-permute-start | bytes 6291464 | tf_op jit(solution)/shard_map/ppermute | solution.py:239
  665.1 5.9 copy-start.21
  675.6 9.3 %copy-start.32 = (bf16[512,1024]{1,0:T(8,128)(2,1)}, bf16[512,1024]{1,0:T(8,128)(2,1)S(1)}, u32[]{:S(2)}) copy-start(bf16[512,1024]{1,0:T(8,128)(2,1)S(1)} %select_convert_fusion.2) | copy-start | bytes 3145732
  675.6 47.2 %collective-permute-start.23 = (bf16[512,1024]{1,0:T(8,128)(2,1)S(1)}, bf16[512,1024]{1,0:T(8,128)(2,1)}, u32[]{:S(2)}, u32[]{:S(2)}) collective-permute-start(bf16[512,1024]{1,0:T(8,128)(2,1)S(1)} %select_convert_fusion.2), channel_id=1, source_target_pairs={{0,1},{1,0},{2,3},{3,2},{4,5},{5,4},{6,7},{7,6},{8,9},{9,8},{10,11... | collective-permute-start | bytes 3145736 | tf_op jit(solution)/shard_map/ppermute | solution.py:239
  684.9 38.0 %copy-start.17 = (bf16[1536,1024]{1,0:T(8,128)(2,1)S(1)}, bf16[1536,1024]{1,0:T(8,128)(2,1)}, u32[]{:S(2)}) copy-start(bf16[1536,1024]{1,0:T(8,128)(2,1)} %pick_rows.11) | copy-start | bytes 9437188
  736.4 7.5 copy-start.9
  738.8 5.2 copy-start.11
  761.7 85.1 %copy-start.12 = (bf16[1,1024,512]{1,2,0:T(8,128)(2,1)S(1)}, bf16[1,1024,512]{1,2,0:T(8,128)(2,1)}, u32[]{:S(2)}) copy-start(bf16[1,1024,512]{1,2,0:T(8,128)(2,1)} %copy.25) | copy-start | bytes 3145732
  (21 other events, 52.0 us)
Sparse Core Ops, SparseCore 0:
  10.1 87.0 all-gather.14
  98.8 160.2 all-gather.8
  260.7 122.3 all-gather.12
  384.5 194.5 all-gather.10
  619.0 114.2 reduce-scatter.4
  735.4 111.3 reduce-scatter.2
